TPU v7x, 768 devices: a whole 4x8x12 slice. The times are simulated.
768 devices in a mesh: rows: 32 (over y, z_hi, core), feat: 24 (over x, z_lo).
Axes of the slice: x: 4, y: 8, z: 12 (z_hi: 2, z_lo: 6; z = z_hi * 6 + z_lo), core: 2. Of those that a mesh axis runs over, the one named last changes fastest.
Arguments:
- features: bfloat16 [393216, 512], P(('rows', 'feat')), may hold values from -6 to 6
- weight: bfloat16 [512, 512], replicated, may hold values from -0.25 to 0.25
- layer_bias: float32 [512], replicated, may hold values from -3 to 3
- block_cols: int32 [3072, 6], P(('rows', 'feat')), may hold values from 0 to 3071, as said below
- neighbours: int32 [393216, 30], P(('rows', 'feat')), may hold values from 0 to 767
- row_counts: int32 [393216], P(('rows', 'feat')), may hold values from 1 to 30
- out_grad: bfloat16 [393216, 512], P(('rows', 'feat')), may hold values from -6 to 6
Outputs:
- hidden: bfloat16 [393216, 512], P(('rows', 'feat'))
- input_grad: bfloat16 [393216, 512], P(('rows', 'feat'))
- weight_grad: float32 [512, 512], P('rows')
- bias_grad: float32 [512], P('rows')
Inputs may be any that keep to these rules, and one draw needn't show every extreme that they name: `block_cols`: block row t is node rows 128 * t to 128 * t + 127. With g = (t // 4) * 4: slot 0 is t itself, slot 1 lies in tiles g - 4 to g - 1, slot 2 in tiles g + 4 to g + 2 * 4 - 1, and every slot in tiles g - 4 to g + 2 * 4 - 1, all taken modulo 3072. `neighbours`: entries at positions row_counts or later are unused.
All inputs are finite; a program needn't handle non-finite values.
Results may differ from a plain program's by a relative error of at most 0.0095.
Values may be sent and summed in bfloat16 or wider, within the bound.
No kernel may reach another device: no remote copies, remote signals or barrier semaphores. Data moves between devices by JAX's collectives and lax.ppermute only.
A program may use at most 64 MiB of HBM per device.

v0:
```python
import math

import jax
import jax.numpy as jnp
from jax import lax
from jax.sharding import PartitionSpec as P

precise = lax.Precision.HIGHEST


def extended(array, sides, width):
    for axis, dim in sides:
        peers, length = (lax.axis_size(axis), array.shape[dim])
        up = [(i, (i + 1) % peers) for i in range(peers)]
        down = [(j, i) for i, j in up]
        last = lax.slice_in_dim(array, length - width, length, axis=dim)
        initial = lax.slice_in_dim(array, 0, width, axis=dim)
        before = lax.ppermute(last, axis, up)
        after = lax.ppermute(initial, axis, down)
        array = jnp.concatenate([before, array, after], axis=dim)
    return array


def from_behind(block, axis, distance):
    devices = range(lax.axis_size(axis))
    route = [((i - distance) % len(devices), i) for i in devices]
    return lax.ppermute(block, axis, route)


def strip_counts(neighbours, row_counts, strip_width):
    columns = jnp.arange(strip_width, dtype=jnp.int32)
    slot_ids = jnp.arange(neighbours.shape[1], dtype=jnp.int32)
    live_slot = slot_ids[None, :] < row_counts[:, None]
    matches = (neighbours[:, :, None] == columns[None, None, :]) & live_slot[:, :, None]
    return jnp.sum(matches.astype(jnp.int32), axis=1).astype(jnp.bfloat16)


def local(features, weight, layer_bias, block_cols, neighbours, row_counts, out_grad):
    rows_dev = features.shape[0]
    feat_width = features.shape[1]
    tile_count = block_cols.shape[0]
    tile_rows = rows_dev // tile_count
    slot_count = block_cols.shape[1]
    devices = lax.axis_size("rows") * lax.axis_size("feat")
    all_tiles = tile_count * devices
    normaliser = 1.0 / math.sqrt(rows_dev * devices)
    own_start = lax.axis_index(("rows", "feat")) * tile_count
    window_start = own_start - tile_count
    local_slot = jnp.mod(block_cols - window_start, all_tiles)
    inverse_root = lax.rsqrt(1.0 + row_counts.astype(jnp.float32))[:, None]
    projected = jnp.dot(features, weight, preferred_element_type=jnp.float32)
    proj_scaled = (projected * inverse_root).astype(jnp.bfloat16)
    window = extended(proj_scaled, ((("rows", "feat"), 0),), rows_dev)
    window_tiles = window.reshape(3 * tile_count, tile_rows, feat_width)
    strips = []
    aggregated = []
    for tile_index in range(tile_count):
        lower_row = tile_index * tile_rows
        count_strip = strip_counts(
            neighbours[lower_row : lower_row + tile_rows],
            row_counts[lower_row : lower_row + tile_rows],
            slot_count * tile_rows,
        )
        sources = jnp.take(window_tiles, local_slot[tile_index], axis=0).reshape(
            slot_count * tile_rows, feat_width
        )
        aggregated.append(jnp.dot(count_strip, sources, preferred_element_type=jnp.float32))
        strips.append(count_strip)
    summed = jnp.concatenate(aggregated, axis=0)
    pre_activation = inverse_root * (summed + proj_scaled.astype(jnp.float32)) + layer_bias[None, :]
    sigmoid_gate = jax.nn.sigmoid(pre_activation)
    hidden = (pre_activation * sigmoid_gate).astype(jnp.bfloat16)
    grad_pre = (
        out_grad.astype(jnp.float32) * sigmoid_gate * (1.0 + pre_activation * (1.0 - sigmoid_gate))
    )
    grad_scaled = (grad_pre * inverse_root).astype(jnp.bfloat16)
    pieces = []
    for tile_index in range(tile_count):
        lower_row = tile_index * tile_rows
        pieces.append(
            lax.dot_general(
                strips[tile_index],
                grad_scaled[lower_row : lower_row + tile_rows],
                (((0,), (0,)), ((), ())),
                preferred_element_type=jnp.float32,
            )
        )
    spread = jnp.stack(pieces).reshape(tile_count * slot_count, tile_rows * feat_width)
    window_ids = jnp.arange(3 * tile_count, dtype=jnp.int32)
    owner_table = (local_slot.reshape(-1)[None, :] == window_ids[:, None]).astype(jnp.float32)
    returned = jnp.dot(owner_table, spread, precision=precise).reshape(3 * rows_dev, feat_width)
    left_part = returned[:rows_dev]
    own_part = returned[rows_dev : 2 * rows_dev]
    right_part = returned[2 * rows_dev :]
    from_right = from_behind(left_part, ("rows", "feat"), -1)
    from_left = from_behind(right_part, ("rows", "feat"), 1)
    incoming = own_part + from_right + from_left
    grad_proj = (inverse_root * (incoming + grad_scaled.astype(jnp.float32))).astype(jnp.bfloat16)
    input_grad = lax.dot_general(
        grad_proj, weight, (((1,), (1,)), ((), ())), preferred_element_type=jnp.float32
    ).astype(jnp.bfloat16)
    local_weight = lax.dot_general(
        features, grad_proj, (((0,), (0,)), ((), ())), preferred_element_type=jnp.float32
    )
    local_bias = jnp.sum(grad_pre, axis=0)
    total_weight, total_bias = lax.psum((local_weight, local_bias), ("rows", "feat"))
    row_share = feat_width // lax.axis_size("rows")
    row_start = lax.axis_index("rows") * row_share
    part_weight = lax.dynamic_slice_in_dim(total_weight, row_start, row_share, 0)
    part_bias = lax.dynamic_slice_in_dim(total_bias, row_start, row_share, 0)
    return (hidden, input_grad, part_weight * normaliser, part_bias * normaliser)


def solution(mesh):
    in_specs = (
        P(("rows", "feat"), None),
        P(),
        P(),
        P(("rows", "feat"), None),
        P(("rows", "feat"), None),
        P(("rows", "feat")),
        P(("rows", "feat"), None),
    )
    out_specs = (P(("rows", "feat"), None), P(("rows", "feat"), None), P("rows", None), P("rows"))
    return jax.shard_map(local, mesh=mesh, in_specs=in_specs, out_specs=out_specs, check_vma=False)
```

profile of v0, /device:TPU:28, one launch (start us, length us, event | category | flops | bytes accessed | tf_op | source)
XLA Modules:
  0.0 620.1 jit_solution(4868562540663907302)
XLA Ops:
  7.2 0.0 copy-start
  7.2 0.0 all-reduce.2.cloned.1.call-start
  7.2 0.7 add_rsqrt_fusion
  8.0 0.3 copy-done
  8.2 1.5 fusion.4
  9.7 0.0 copy-start.4
  9.7 12.7 %collective-permute-start.1 = (bf16[512,512]{1,0:T(8,128)(2,1)S(1)}, bf16[512,512]{1,0:T(8,128)(2,1)S(1)}, u32[]{:S(2)}, u32[]{:S(2)}) collective-permute-start(bf16[512,512]{1,0:T(8,128)(2,1)S(1)} %fusion.4), channel_id=1, source_target_pairs={{1,0},{2,1},{3,2},{4,3},{5,4},{6,5},{7,6},{8,7},{9,8},{10,9},{11,1... | collective-permute-start | bytes 1572872 | tf_op jit(solution)/shard_map/ppermute | solution.py:19
  22.4 1.9 collective-permute-start
  24.4 0.7 add_select_fusion
  25.1 0.1 eq.81
  25.2 0.8 fusion.28
  26.1 0.8 fusion.27
  26.9 4.6 convert_reduce_fusion.2
  31.5 5.3 convert_reduce_fusion
  36.8 0.0 collective-permute-done.1
  36.8 0.0 copy-done.4
  36.8 0.8 copy-done.8
  37.6 8.1 %collective-permute-done = bf16[512,512]{1,0:T(8,128)(2,1)} collective-permute-done((bf16[512,512]{1,0:T(8,128)(2,1)S(1)}, bf16[512,512]{1,0:T(8,128)(2,1)}, u32[]{:S(2)}, u32[]{:S(2)}) %collective-permute-start) | collective-permute-done | bytes 524320 | tf_op jit(solution)/shard_map/ppermute | solution.py:18
  45.7 1.5 pad_maximum_fusion.1
  47.1 1.5 gather_fusion.3
  48.7 1.5 gather_fusion.2
  50.2 1.5 gather_fusion.1
  51.7 1.5 gather_fusion
  53.2 1.7 broadcast_select_fusion
  54.9 0.0 copy-done.1
  54.9 0.3 fusion.12
  55.2 0.3 fusion.15
  55.5 0.0 copy-done.2
  55.5 0.0 copy-done.3
  55.5 0.0 copy-start.5
  55.5 0.0 copy-start.7
  55.5 0.0 copy-start.9
  55.5 0.2 broadcast_select_fusion.2
  55.8 0.3 fusion.18
  56.0 0.3 fusion.21
  56.3 0.2 copy-done.5
  56.5 0.2 copy-done.7
  56.7 0.0 copy-done.9
  56.7 1.4 fusion.25
  58.1 0.1 multiply_convert_fusion.1
  58.3 0.4 convolution_bitcast_fusion
  58.7 0.4 convolution_bitcast_fusion.1
  59.1 0.4 convolution_bitcast_fusion.2
  59.5 0.4 convolution_bitcast_fusion.3
  59.8 2.9 pad_maximum_fusion
  62.8 6.8 %reshape.131 = f32[24,65536]{1,0:T(8,128)} reshape(f32[4,768,512]{2,1,0:T(8,128)} %pad_maximum_fusion) | data formatting | bytes 12582912 | tf_op jit(solution)/shard_map/reshape | solution.py:88
  69.6 4.6 fusion.23
  74.3 1.8 fusion.26
  76.1 2.9 slice.85
  79.0 3.0 slice.87
  81.9 3.7 collective-permute-start.3
  85.6 7.9 %collective-permute-start.2 = (f32[512,512]{1,0:T(8,128)}, f32[512,512]{1,0:T(8,128)}, u32[]{:S(2)}, u32[]{:S(2)}) collective-permute-start(f32[512,512]{1,0:T(8,128)} %slice.85), channel_id=1, source_target_pairs={{1,0},{2,1},{3,2},{4,3},{5,4},{6,5},{7,6},{8,7},{9,8},{10,9},{11,1... | collective-permute-start | bytes 3145736 | tf_op jit(solution)/shard_map/ppermute | solution.py:27
  93.5 1.7 slice.83
  95.2 20.8 %collective-permute-done.3 = f32[512,512]{1,0:T(8,128)} collective-permute-done((f32[512,512]{1,0:T(8,128)}, f32[512,512]{1,0:T(8,128)}, u32[]{:S(2)}, u32[]{:S(2)}) %collective-permute-start.3) | collective-permute-done | bytes 1048608 | tf_op jit(solution)/shard_map/ppermute | solution.py:27
  116.0 18.2 %collective-permute-done.2 = f32[512,512]{1,0:T(8,128)} collective-permute-done((f32[512,512]{1,0:T(8,128)}, f32[512,512]{1,0:T(8,128)}, u32[]{:S(2)}, u32[]{:S(2)}) %collective-permute-start.2) | collective-permute-done | bytes 1048608 | tf_op jit(solution)/shard_map/ppermute | solution.py:27
  134.1 2.1 multiply_convert_fusion
  136.2 1.5 convolution_bitcast_fusion.4
  137.7 0.0 all-reduce.2.cloned.1.call-update
  137.7 107.0 %psum.15 = f32[512]{0:T(512)S(1)} all-reduce(f32[512]{0:T(512)S(1)} %get-tuple-element.13), channel_id=1, replica_groups=mesh['rows'=32,'feat'=24] {'rows','feat'}, use_global_device_ids=true, to_apply=%region_6.8 | all-reduce | flops 512 | bytes 4096 | tf_op jit(solution)/shard_map/psum | solution.py:106
  244.7 0.6 dynamic-slice_multiply_fusion.1
  245.3 1.3 convolution_convert_fusion
  246.6 364.9 %all-reduce.2.cloned.1.call-done = f32[512,512]{0,1:T(8,128)} async-done(((f32[512,512]{0,1:T(8,128)}), f32[512,512]{0,1:T(8,128)}) %all-reduce.2.cloned.1.call-update) | async-done | bytes 1048592 | tf_op jit(solution)/shard_map/psum | solution.py:106
  611.5 1.1 dynamic-slice_multiply_fusion
  612.6 0.7 copy.16
  (15 shorter events, 0.1 us)
Async XLA Ops:
  7.2 1.1 copy-start
  7.2 604.3 %all-reduce.2.cloned.1.call-start = ((), (), s32[]{:S(2)}) async-start(), calls=%async_computation | async-start | bytes 2097152 | tf_op jit(solution)/shard_map/psum | solution.py:106
  9.7 27.1 %copy-start.4 = (bf16[512,512]{1,0:T(8,128)(2,1)}, bf16[512,512]{1,0:T(8,128)(2,1)S(1)}, u32[]{:S(2)}) copy-start(bf16[512,512]{1,0:T(8,128)(2,1)S(1)} %fusion.4) | copy-start | bytes 1572868
  9.7 27.1 %collective-permute-start.1 = (bf16[512,512]{1,0:T(8,128)(2,1)S(1)}, bf16[512,512]{1,0:T(8,128)(2,1)S(1)}, u32[]{:S(2)}, u32[]{:S(2)}) collective-permute-start(bf16[512,512]{1,0:T(8,128)(2,1)S(1)} %fusion.4), channel_id=1, source_target_pairs={{1,0},{2,1},{3,2},{4,3},{5,4},{6,5},{7,6},{8,7},{9,8},{10,9},{11,1... | collective-permute-start | bytes 1572872 | tf_op jit(solution)/shard_map/ppermute | solution.py:19
  22.4 23.2 %collective-permute-start = (bf16[512,512]{1,0:T(8,128)(2,1)S(1)}, bf16[512,512]{1,0:T(8,128)(2,1)}, u32[]{:S(2)}, u32[]{:S(2)}) collective-permute-start(bf16[512,512]{1,0:T(8,128)(2,1)S(1)} %fusion.4), channel_id=1, source_target_pairs={{0,1},{1,2},{2,3},{3,4},{4,5},{5,6},{6,7},{7,8},{8,9},{9,10},{10,1... | collective-permute-start | bytes 1572872 | tf_op jit(solution)/shard_map/ppermute | solution.py:18
  36.8 0.8 copy-start.8
  53.2 1.7 copy-start.1
  53.2 2.3 copy-start.2
  53.2 2.3 copy-start.3
  55.5 1.0 copy-start.5
  55.5 1.2 copy-start.7
  55.5 1.2 copy-start.9
  81.9 34.0 %collective-permute-start.3 = (f32[512,512]{1,0:T(8,128)}, f32[512,512]{1,0:T(8,128)}, u32[]{:S(2)}, u32[]{:S(2)}) collective-permute-start(f32[512,512]{1,0:T(8,128)} %slice.87), channel_id=1, source_target_pairs={{767,0},{0,1},{1,2},{2,3},{3,4},{4,5},{5,6},{6,7},{7,8},{8,9},{9,1... | collective-permute-start | bytes 3145736 | tf_op jit(solution)/shard_map/ppermute | solution.py:27
  85.6 48.5 %collective-permute-start.2 = (f32[512,512]{1,0:T(8,128)}, f32[512,512]{1,0:T(8,128)}, u32[]{:S(2)}, u32[]{:S(2)}) collective-permute-start(f32[512,512]{1,0:T(8,128)} %slice.85), channel_id=1, source_target_pairs={{1,0},{2,1},{3,2},{4,3},{5,4},{6,5},{7,6},{8,7},{9,8},{10,9},{11,1... | collective-permute-start | bytes 3145736 | tf_op jit(solution)/shard_map/ppermute | solution.py:27
  95.2 150.1 %copy-start.6 = (bf16[512,512]{1,0:T(8,128)(2,1)S(1)}, bf16[512,512]{1,0:T(8,128)(2,1)}, u32[]{:S(2)}) copy-start(bf16[512,512]{1,0:T(8,128)(2,1)} %param.10) | copy-start | bytes 1572868
Sparse Core Ops, SparseCore 0:
  137.8 473.5 all-reduce.1
where the time goes:
time: 621 us; the launch traced here: 620 us
  waiting for transfers between devices  412 us (66%)
  blocking collectives  107 us (17%)
  local copies, waits for them, and re-layouts  26.2 us (4%)
  starting transfers between devices  26.2 us (4%)
  other arithmetic  23 us (4%)
  between operations  14.3 us (2%)
  matrix products  11.5 us (2%)
    psum x1, waiting for transfers between devices, local(): lax.psum((local_weight, local_bias), ('rows', 'feat'))  365 us
    psum x1, blocking collectives, local(): lax.psum((local_weight, local_bias), ('rows', 'feat'))  107 us
    ppermute x2, waiting for transfers between devices, from_behind(): return lax.ppermute(block, axis, route)  38.9 us
    ppermute x1, starting transfers between devices, extended(): after = lax.ppermute(initial, axis, down)  12.7 us
  transfers between devices with their start and end apart: 5, of which 4 were waited for; matrix products, arithmetic and copies ran while one was open for 3% of the time, Pallas kernels for 0%

commit v1 on v0

v1 whole, which is shorter than its diff:
```python
import math

import jax
import jax.numpy as jnp
from jax import lax
from jax.experimental import pallas as pl
from jax.experimental.pallas import tpu as pltpu
from jax.sharding import Mesh
from jax.sharding import PartitionSpec as P

AXES = ("y", "zh", "core", "x", "zl")
SIZES = (8, 2, 2, 4, 6)
NODE = AXES
BITS = 5
f32 = jnp.float32
bf16 = jnp.bfloat16


def permute(array, axes, route):
    peers = lax.axis_size(axes)
    return lax.ppermute(array, axes, [(i, route(i) % peers) for i in range(peers)])


def rows_dot(a, b):
    return jnp.dot(a, b, preferred_element_type=f32)


def transposed_dot(a, b):
    return lax.dot_general(a, b, (((0,), (0,)), ((), ())), preferred_element_type=f32)


def adjacency_kernel(slot_ref, nbr_ref, cnt_ref, adj_ref, adjt_ref):
    tile = pl.program_id(0)
    rows, width = nbr_ref.shape
    slots = slot_ref.shape[1]
    tiles = adj_ref.shape[1] // rows
    own_first = tiles // 3
    nbr = nbr_ref[...]
    live = lax.broadcasted_iota(jnp.int32, nbr.shape, 1) < cnt_ref[...]
    low = jnp.bitwise_and(nbr, rows - 1)
    shift = BITS * lax.shift_right_logical(nbr, rows.bit_length() - 1)
    step = jnp.where(live, lax.shift_left(jnp.ones_like(nbr), shift), 0)
    lane = lax.broadcasted_iota(jnp.int32, (rows, rows), 1)
    packed = jnp.zeros((rows, rows), jnp.int32)
    for k in range(width):
        packed += jnp.where(lane == low[:, k : k + 1], step[:, k : k + 1], 0)
    adj_ref[...] = jnp.zeros_like(adj_ref)
    row = lax.broadcasted_iota(jnp.int32, (rows, rows), 0)
    own = pl.ds(pl.multiple_of((own_first + tile) * rows, rows), rows)
    adj_ref[:, own] = (row == lane).astype(f32).astype(bf16)
    for s in range(slots):
        counts = jnp.bitwise_and(lax.shift_right_logical(packed, BITS * s), 2**BITS - 1)
        place = pl.ds(pl.multiple_of(slot_ref[tile, s] * rows, rows), rows)
        adj_ref[:, place] += counts.astype(f32).astype(bf16)
    adjt_ref[...] = adj_ref[...].T


def build_adjacency(local_slot, neighbours, counts):
    tiles, slots = local_slot.shape
    nodes, width = neighbours.shape
    rows = nodes // tiles
    window = 3 * nodes
    return pl.pallas_call(
        adjacency_kernel,
        grid=(tiles,),
        in_specs=[
            pl.BlockSpec(memory_space=pltpu.SMEM),
            pl.BlockSpec((rows, width), lambda t: (t, 0)),
            pl.BlockSpec((rows, 1), lambda t: (t, 0)),
        ],
        out_specs=[
            pl.BlockSpec((rows, window), lambda t: (t, 0)),
            pl.BlockSpec((window, rows), lambda t: (0, t)),
        ],
        out_shape=[
            jax.ShapeDtypeStruct((nodes, window), bf16),
            jax.ShapeDtypeStruct((window, nodes), bf16),
        ],
        cost_estimate=pl.CostEstimate(flops=10**9, bytes_accessed=8 * 10**6, transcendentals=0),
        name="adjacency",
    )(local_slot, neighbours, counts)


def middle_kernel(
    core_ref, adj, adjt, own, left, right, weight, bias, root, grad,
    hidden, wsend, wkeep, part_left, part_right, part_own, agg_s, scaled_s, pre_s,
):
    nodes, width = own.shape
    rows = 128
    for first in range(0, nodes, rows):
        r = pl.ds(first, rows)
        agg = rows_dot(adj[r, 0:nodes], left[...])
        agg += rows_dot(adj[r, nodes : 2 * nodes], own[...])
        agg += rows_dot(adj[r, 2 * nodes : 3 * nodes], right[...])
        agg = agg.astype(bf16)
        agg_s[r, :] = agg
        pre = root[r, :] * rows_dot(agg, weight[...]) + bias[...]
        gate = jax.nn.sigmoid(pre)
        hidden[r, :] = (pre * gate).astype(bf16)
        grad_pre = grad[r, :].astype(f32) * gate * (1.0 + pre * (1.0 - gate))
        pre_s[r, :] = grad_pre.astype(bf16)
        scaled_s[r, :] = (grad_pre * root[r, :]).astype(bf16)
    scaled = scaled_s[...]
    core = core_ref[0]
    ones = jnp.ones((nodes, 128), bf16)
    wgrad = transposed_dot(agg_s[...], scaled).astype(bf16)
    bgrad = transposed_dot(pre_s[...], ones).astype(bf16)
    share = 16
    for chunk in range(width // share):
        outer, side = divmod(chunk, 2)
        band = slice(chunk * share, (chunk + 1) * share)
        place = pl.ds(outer * share, share)

        @pl.when(core == side)
        def _():
            wkeep[place, 0:width] = wgrad[band]
            wkeep[place, width : width + 128] = bgrad[band]

        @pl.when(core != side)
        def _():
            wsend[place, 0:width] = wgrad[band]
            wsend[place, width : width + 128] = bgrad[band]

    part_left[...] = rows_dot(adjt[0:nodes, :], scaled).astype(bf16)
    part_right[...] = rows_dot(adjt[2 * nodes : 3 * nodes, :], scaled).astype(bf16)
    part_own[...] = rows_dot(adjt[nodes : 2 * nodes, :], scaled)


def middle(core, adj, adjt, own, left, right, weight, bias, root, grad):
    nodes, width = own.shape
    half = jax.ShapeDtypeStruct((width // 2, width + 128), bf16)
    square = jax.ShapeDtypeStruct((nodes, width), bf16)
    vmem = pl.BlockSpec(memory_space=pltpu.VMEM)
    return pl.pallas_call(
        middle_kernel,
        in_specs=[pl.BlockSpec(memory_space=pltpu.SMEM)] + [vmem] * 9,
        out_specs=[vmem] * 6,
        out_shape=[square, half, half, square, square, jax.ShapeDtypeStruct((nodes, width), f32)],
        scratch_shapes=[pltpu.VMEM((nodes, width), bf16)] * 3,
        cost_estimate=pl.CostEstimate(flops=2 * 10**9, bytes_accessed=10**7, transcendentals=0),
        name="middle",
    )(core, adj, adjt, own, left, right, weight, bias, root, grad)


def final_kernel(part_own, from_left, from_right, root, weight, out):
    nodes = out.shape[0]
    rows = 128
    for first in range(0, nodes, rows):
        r = pl.ds(first, rows)
        total = part_own[r, :] + from_left[r, :].astype(f32) + from_right[r, :].astype(f32)
        grad_proj = (root[r, :] * total).astype(bf16)
        out[r, :] = lax.dot_general(
            grad_proj, weight[...], (((1,), (1,)), ((), ())), preferred_element_type=f32
        ).astype(bf16)


def final(part_own, from_left, from_right, root, weight):
    vmem = pl.BlockSpec(memory_space=pltpu.VMEM)
    return pl.pallas_call(
        final_kernel,
        in_specs=[vmem] * 5,
        out_specs=vmem,
        out_shape=jax.ShapeDtypeStruct(part_own.shape, bf16),
        cost_estimate=pl.CostEstimate(flops=10**8, bytes_accessed=10**6, transcendentals=0),
        name="final",
    )(part_own, from_left, from_right, root, weight)


def local(features, weight, layer_bias, block_cols, neighbours, row_counts, out_grad):
    nodes, width = features.shape
    tile_count = block_cols.shape[0]
    devices = lax.axis_size(NODE)
    all_tiles = tile_count * devices
    normaliser = 1.0 / math.sqrt(nodes * devices)
    window_start = (lax.axis_index(NODE) - 1) * tile_count
    local_slot = jnp.mod(block_cols - window_start, all_tiles)
    counts = row_counts[:, None]
    root = lax.rsqrt(1.0 + counts.astype(f32))
    own = (features.astype(f32) * root).astype(bf16)
    left = permute(own, NODE, lambda i: i + 1)
    right = permute(own, NODE, lambda i: i - 1)
    adj, adjt = build_adjacency(local_slot, neighbours, counts)
    core = lax.axis_index("core").astype(jnp.int32).reshape(1)
    hidden, wsend, wkeep, part_left, part_right, part_own = middle(
        core, adj, adjt, own, left, right, weight, layer_bias[None, :], root, out_grad
    )
    got = permute(wsend, "core", lambda i: i ^ 1)
    from_right = permute(part_left, NODE, lambda i: i - 1)
    from_left = permute(part_right, NODE, lambda i: i + 1)

    ny, nzh = lax.axis_size("y"), lax.axis_size("zh")
    share = width // (ny * nzh * lax.axis_size("core"))
    chip = (wkeep.astype(f32) + got.astype(f32)).astype(bf16)
    chip = chip.reshape(ny, nzh * share, width + 128)
    column = jnp.sum(lax.all_to_all(chip, "y", 0, 0).astype(f32), axis=0)
    high = lax.axis_index("zh")
    kept = jnp.where(high == 0, column[:share], column[share:])
    sent = jnp.where(high == 0, column[share:], column[:share]).astype(bf16)
    pair = kept + permute(sent, ("zh", "zl"), lambda i: -1 - i).astype(f32)
    spread = lax.axis_size(("x", "zl"))
    every = jnp.broadcast_to(pair.astype(bf16)[None], (spread, share, width + 128))
    total = jnp.sum(lax.all_to_all(every, ("x", "zl"), 0, 0).astype(f32), axis=0) * normaliser

    input_grad = final(part_own, from_left, from_right, root, weight)
    return (hidden, input_grad, total[:, :width], total[:, width])


def solution(mesh):
    wide = Mesh(mesh.devices.reshape(SIZES), AXES)
    row = P(NODE, None)
    in_specs = (row, P(), P(), row, row, P(NODE), row)
    shares = ("y", "zh", "core")
    out_specs = (row, row, P(shares, None), P(shares))
    return jax.shard_map(local, mesh=wide, in_specs=in_specs, out_specs=out_specs, check_vma=False)
```

time: 621 us -> 137 us (0.22)
  the two profiles are of different devices: /device:TPU:28 before, /device:TPU:128 now
where the time goes in v1:
time: 137 us; the launch traced here: 136 us
  waiting for transfers between devices  57.6 us (42%)
  starting transfers between devices  47.7 us (35%)
  Pallas kernels  18.1 us (13%)
  local copies, waits for them, and re-layouts  7.18 us (5%)
  other arithmetic  4.48 us (3%)
    ppermute x6, waiting for transfers between devices, permute(): lax.ppermute(array, axes, [(i, route(i) % peers) for i in range(peers)])  44 us
    ppermute x6, starting transfers between devices, permute(): lax.ppermute(array, axes, [(i, route(i) % peers) for i in range(peers)])  27 us
    all_to_all x1, starting transfers between devices, local(): lax.all_to_all(every, ('x', 'zl'), 0, 0).astype(f32)  15.3 us
    all_to_all x1, waiting for transfers between devices, local(): column = jnp.sum(lax.all_to_all(chip, 'y', 0, 0).astype(f32), axis=0)  13.6 us
    pallas_call x1, Pallas kernels, build_adjacency(): pl.pallas_call(adjacency_kernel, grid=(tiles,), in_specs=[pl.BlockSpec(me...  7.5 us
    pallas_call x1, Pallas kernels, middle(): pl.pallas_call(middle_kernel, in_specs=[pl.BlockSpec(memory_space=pltpu.S...  7.27 us
    all_to_all x1, starting transfers between devices, local(): column = jnp.sum(lax.all_to_all(chip, 'y', 0, 0).astype(f32), axis=0)  5.42 us
    pallas_call x1, Pallas kernels, final(): pl.pallas_call(final_kernel, in_specs=[vmem] * 5, out_specs=vmem, out_sha...  3.38 us
  transfers between devices with their start and end apart: 8, of which 6 were waited for; matrix products, arithmetic and copies ran while one was open for 3% of the time, Pallas kernels for 8%

profile of v1, /device:TPU:128, one launch (start us, length us, event | category | flops | bytes accessed | tf_op | source)
XLA Modules:
  0.0 136.0 jit_solution(17098254426450640307)
XLA Ops:
  0.6 0.0 copy-start.3
  0.6 0.0 copy-start.4
  0.7 0.7 add_rsqrt_fusion
  1.4 1.2 multiply_convert_fusion.own
  2.6 0.0 copy-start
  2.6 1.9 %collective-permute-start.1 = (bf16[512,512]{1,0:T(8,128)(2,1)S(1)}, bf16[512,512]{1,0:T(8,128)(2,1)S(1)}, u32[]{:S(2)}, u32[]{:S(2)}) collective-permute-start(bf16[512,512]{1,0:T(8,128)(2,1)S(1)} %multiply_convert_fusion.own), channel_id=1, source_target_pairs={{0,767},{1,0},{2,1},{3,2},{4,3},{5,4},{6,5},{7,6},{8,7},{9,8},{10,... | collective-permute-start | bytes 1572872 | tf_op jit(solution)/shard_map/ppermute | solution.py:21
  4.5 4.3 %collective-permute-start = (bf16[512,512]{1,0:T(8,128)(2,1)S(1)}, bf16[512,512]{1,0:T(8,128)(2,1)S(1)}, u32[]{:S(2)}, u32[]{:S(2)}) collective-permute-start(bf16[512,512]{1,0:T(8,128)(2,1)S(1)} %multiply_convert_fusion.own), channel_id=1, source_target_pairs={{0,1},{1,2},{2,3},{3,4},{4,5},{5,6},{6,7},{7,8},{8,9},{9,10},{10,1... | collective-permute-start | bytes 1572872 | tf_op jit(solution)/shard_map/ppermute | solution.py:21
  8.9 0.9 copy.18.root
  9.7 1.7 %copy.16.nbr_ref = s32[512,30]{1,0:T(8,128)} copy(s32[512,30]{0,1:T(8,128)} %param.11) | data formatting | bytes 122880 | tf_op args[4]
  11.4 0.0 copy-done.3
  11.4 0.9 copy.17.cnt_ref
  12.3 0.0 copy-done.4
  12.3 0.6 add_select_fusion.slot_ref
  12.9 7.5 %adjacency.1 = (bf16[512,1536]{1,0:T(8,128)(2,1)}, bf16[1536,512]{1,0:T(8,128)(2,1)}) custom-call(s32[4,6]{1,0:T(4,128)} %add_select_fusion.slot_ref, s32[512,30]{1,0:T(8,128)} %copy.16.nbr_ref, s32[512,1]{1,0:T(8,128)} %copy.17.cnt_ref), custom_call_target="tpu_custom_call" | custom-call | flops 1000000000 | bytes 8000000 | tf_op jit(solution)/shard_map/adjacency/pallas_call | solution.py:63
  20.4 0.0 copy-done
  20.4 0.0 collective-permute-done.1.right
  20.4 0.0 copy-start.5
  20.4 7.2 %collective-permute-done.left = bf16[512,512]{1,0:T(8,128)(2,1)S(1)} collective-permute-done((bf16[512,512]{1,0:T(8,128)(2,1)S(1)}, bf16[512,512]{1,0:T(8,128)(2,1)S(1)}, u32[]{:S(2)}, u32[]{:S(2)}) %collective-permute-start) | collective-permute-done | bytes 524320 | tf_op jit(solution)/shard_map/ppermute | solution.py:21
  27.5 0.0 copy-start.6
  27.5 0.0 copy-done.5
  27.5 0.8 copy-done.6
  28.4 7.3 %middle.1 = (bf16[512,512]{1,0:T(8,128)(2,1)}, bf16[256,640]{1,0:T(8,128)(2,1)}, bf16[256,640]{1,0:T(8,128)(2,1)}, bf16[512,512]{1,0:T(8,128)(2,1)}, bf16[512,512]{1,0:T(8,128)(2,1)}, /*index=5*/f32[512,512]{1,0:T(8,128)}) custom-call(s32[1]{0:T(128)} %bitcast.core_ref, bf16[512,1536]{1,0:T(8,128)(2,1)} %get-tuple-element.12.adj, ...), custom_call_target="tpu_custom_call" | custom-call | flops 2000000000 | bytes 10000000 | tf_op jit(solution)/shard_map/middle/pallas_call | solution.py:134
  35.6 1.9 %collective-permute-start.4 = (bf16[256,640]{1,0:T(8,128)(2,1)}, bf16[256,640]{1,0:T(8,128)(2,1)S(1)}, u32[]{:S(2)}, u32[]{:S(2)}) collective-permute-start(bf16[256,640]{1,0:T(8,128)(2,1)} %get-tuple-element.19), channel_id=1, source_target_pairs={{0,24},{24,0},{1,25},{25,1},{2,26},{26,2},{3,27},{27,3},{4,28},{28... | collective-permute-start | bytes 983048 | tf_op jit(solution)/shard_map/ppermute | solution.py:21
  37.6 1.8 %collective-permute-done.4 = bf16[256,640]{1,0:T(8,128)(2,1)S(1)} collective-permute-done((bf16[256,640]{1,0:T(8,128)(2,1)}, bf16[256,640]{1,0:T(8,128)(2,1)S(1)}, u32[]{:S(2)}, u32[]{:S(2)}) %collective-permute-start.4) | collective-permute-done | bytes 327712 | tf_op jit(solution)/shard_map/ppermute | solution.py:21
  39.4 1.8 %add_convert_fusion = bf16[256,640]{1,0:T(8,128)(2,1)} fusion(bf16[256,640]{1,0:T(8,128)(2,1)S(1)} %collective-permute-done.4, bf16[256,640]{1,0:T(8,128)(2,1)} %get-tuple-element.18), kind=kLoop, calls=%fused_computation.3 | loop fusion | flops 655360 | bytes 983040 | tf_op jit(solution)/shard_map/convert_element_type | solution.py:193
  41.2 0.0 copy-start.8
  41.2 0.0 copy-start.7
  41.2 5.4 %all-to-all-start = ((bf16[8,32,640]{2,1,0:T(8,128)(2,1)}), bf16[8,32,640]{2,1,0:T(8,128)(2,1)S(1)}, u32[]{:S(2)}, u32[]{:S(2)}) async-start(bf16[8,32,640]{2,1,0:T(8,128)(2,1)} %bitcast.4), calls=%async_computation | async-start | bytes 655360 | tf_op jit(solution)/shard_map/all_to_all | solution.py:195
  46.6 13.6 %all-to-all-done = bf16[8,32,640]{2,1,0:T(8,128)(2,1)S(1)} async-done(((bf16[8,32,640]{2,1,0:T(8,128)(2,1)}), bf16[8,32,640]{2,1,0:T(8,128)(2,1)S(1)}, u32[]{:S(2)}, u32[]{:S(2)}) %all-to-all-start) | async-done | bytes 327712 | tf_op jit(solution)/shard_map/all_to_all | solution.py:195
  60.2 13.0 %collective-permute-start.5 = (bf16[16,640]{1,0:T(8,128)(2,1)S(1)}, bf16[16,640]{1,0:T(8,128)(2,1)S(1)}, u32[]{:S(2)}, u32[]{:S(2)}) collective-permute-start(bf16[16,640]{1,0:T(8,128)(2,1)S(1)} %select_convert_fusion), channel_id=1, source_target_pairs={{0,53},{1,52},{2,51},{3,50},{4,49},{5,48},{48,5},{49,4},{50,3},{51... | collective-permute-start | bytes 61448 | tf_op jit(solution)/shard_map/ppermute | solution.py:21
  73.3 1.7 %collective-permute-done.5 = bf16[16,640]{1,0:T(8,128)(2,1)S(1)} collective-permute-done((bf16[16,640]{1,0:T(8,128)(2,1)S(1)}, bf16[16,640]{1,0:T(8,128)(2,1)S(1)}, u32[]{:S(2)}, u32[]{:S(2)}) %collective-permute-start.5) | collective-permute-done | bytes 20512 | tf_op jit(solution)/shard_map/ppermute | solution.py:21
  75.0 0.9 broadcast_in_dim.14
  75.9 15.3 %all-to-all-start.1 = ((bf16[24,16,640]{2,1,0:T(8,128)(2,1)}), bf16[24,16,640]{2,1,0:T(8,128)(2,1)S(1)}, u32[]{:S(2)}, u32[]{:S(2)}) async-start(bf16[24,16,640]{2,1,0:T(8,128)(2,1)} %broadcast_in_dim.14), calls=%async_computation.1 | async-start | bytes 983040 | tf_op jit(solution)/shard_map/all_to_all | solution.py:202
  91.2 0.0 copy-done.8
  91.2 3.4 %collective-permute-start.2 = (bf16[512,512]{1,0:T(8,128)(2,1)S(1)}, bf16[512,512]{1,0:T(8,128)(2,1)S(1)}, u32[]{:S(2)}, u32[]{:S(2)}) collective-permute-start(bf16[512,512]{1,0:T(8,128)(2,1)S(1)} %copy-done.8), channel_id=1, source_target_pairs={{0,1},{1,2},{2,3},{3,4},{4,5},{5,6},{6,7},{7,8},{8,9},{9,10},{10,1... | collective-permute-start | bytes 1572872 | tf_op jit(solution)/shard_map/ppermute | solution.py:21
  94.6 0.0 copy-done.7
  94.6 2.5 %collective-permute-start.3 = (bf16[512,512]{1,0:T(8,128)(2,1)S(1)}, bf16[512,512]{1,0:T(8,128)(2,1)S(1)}, u32[]{:S(2)}, u32[]{:S(2)}) collective-permute-start(bf16[512,512]{1,0:T(8,128)(2,1)S(1)} %copy-done.7), channel_id=1, source_target_pairs={{0,767},{1,0},{2,1},{3,2},{4,3},{5,4},{6,5},{7,6},{8,7},{9,8},{10,... | collective-permute-start | bytes 1572872 | tf_op jit(solution)/shard_map/ppermute | solution.py:21
  97.1 25.8 %collective-permute-done.2.from_left = bf16[512,512]{1,0:T(8,128)(2,1)S(1)} collective-permute-done((bf16[512,512]{1,0:T(8,128)(2,1)S(1)}, bf16[512,512]{1,0:T(8,128)(2,1)S(1)}, u32[]{:S(2)}, u32[]{:S(2)}) %collective-permute-start.2) | collective-permute-done | bytes 524320 | tf_op jit(solution)/shard_map/ppermute | solution.py:21
  122.9 0.0 copy-start.1
  122.9 7.5 %collective-permute-done.3.from_right = bf16[512,512]{1,0:T(8,128)(2,1)S(1)} collective-permute-done((bf16[512,512]{1,0:T(8,128)(2,1)S(1)}, bf16[512,512]{1,0:T(8,128)(2,1)S(1)}, u32[]{:S(2)}, u32[]{:S(2)}) %collective-permute-start.3) | collective-permute-done | bytes 524320 | tf_op jit(solution)/shard_map/ppermute | solution.py:21
  130.4 0.0 copy-start.2
  130.4 0.0 copy-done.1
  130.4 0.8 copy-done.2
  131.2 3.4 %final.1 = bf16[512,512]{1,0:T(8,128)(2,1)} custom-call(f32[512,512]{1,0:T(8,128)} %get-tuple-element.15.part_own, bf16[512,512]{1,0:T(8,128)(2,1)} %copy-done.1, bf16[512,512]{1,0:T(8,128)(2,1)} %copy-done.2, f32[512,1]{1,0:T(8,128)} %copy.18.root, bf16[512,512]{1,0:T(8,128)(2,1)} %weight.3), custom_call_target="tpu_custom_call" | custom-call | flops 100000000 | bytes 1000000 | tf_op jit(solution)/shard_map/final/pallas_call | solution.py:159
  134.6 0.0 all-to-all-done.1
  134.6 0.1 convert_reduce_fusion
  134.7 0.6 slice_reduce_fusion
  135.3 0.6 slice.20
  (4 shorter events, 0.1 us)
Async XLA Ops:
  0.6 10.8 %copy-start.3 = (s32[512]{0:T(512)S(1)}, s32[512]{0:T(512)}, u32[]{:S(2)}) copy-start(s32[512]{0:T(512)} %param.12) | copy-start | bytes 6148
  0.6 11.6 %copy-start.4 = (s32[4,6]{1,0:T(4,128)S(1)}, s32[4,6]{1,0:T(4,128)}, u32[]{:S(2)}) copy-start(s32[4,6]{1,0:T(4,128)} %param.10) | copy-start | bytes 292
  2.6 17.8 %copy-start = (bf16[512,512]{1,0:T(8,128)(2,1)}, bf16[512,512]{1,0:T(8,128)(2,1)S(1)}, u32[]{:S(2)}) copy-start(bf16[512,512]{1,0:T(8,128)(2,1)S(1)} %multiply_convert_fusion.own) | copy-start | bytes 1572868
  2.6 17.8 %collective-permute-start.1 = (bf16[512,512]{1,0:T(8,128)(2,1)S(1)}, bf16[512,512]{1,0:T(8,128)(2,1)S(1)}, u32[]{:S(2)}, u32[]{:S(2)}) collective-permute-start(bf16[512,512]{1,0:T(8,128)(2,1)S(1)} %multiply_convert_fusion.own), channel_id=1, source_target_pairs={{0,767},{1,0},{2,1},{3,2},{4,3},{5,4},{6,5},{7,6},{8,7},{9,8},{10,... | collective-permute-start | bytes 1572872 | tf_op jit(solution)/shard_map/ppermute | solution.py:21
  4.5 23.0 %collective-permute-start = (bf16[512,512]{1,0:T(8,128)(2,1)S(1)}, bf16[512,512]{1,0:T(8,128)(2,1)S(1)}, u32[]{:S(2)}, u32[]{:S(2)}) collective-permute-start(bf16[512,512]{1,0:T(8,128)(2,1)S(1)} %multiply_convert_fusion.own), channel_id=1, source_target_pairs={{0,1},{1,2},{2,3},{3,4},{4,5},{5,6},{6,7},{7,8},{8,9},{9,10},{10,1... | collective-permute-start | bytes 1572872 | tf_op jit(solution)/shard_map/ppermute | solution.py:21
  20.4 7.2 %copy-start.5 = (bf16[512,512]{1,0:T(8,128)(2,1)}, bf16[512,512]{1,0:T(8,128)(2,1)S(1)}, u32[]{:S(2)}) copy-start(bf16[512,512]{1,0:T(8,128)(2,1)S(1)} %collective-permute-done.1.right) | copy-start | bytes 1572868
  27.5 0.8 copy-start.6
  35.6 3.7 %collective-permute-start.4 = (bf16[256,640]{1,0:T(8,128)(2,1)}, bf16[256,640]{1,0:T(8,128)(2,1)S(1)}, u32[]{:S(2)}, u32[]{:S(2)}) collective-permute-start(bf16[256,640]{1,0:T(8,128)(2,1)} %get-tuple-element.19), channel_id=1, source_target_pairs={{0,24},{24,0},{1,25},{25,1},{2,26},{26,2},{3,27},{27,3},{4,28},{28... | collective-permute-start | bytes 983048 | tf_op jit(solution)/shard_map/ppermute | solution.py:21
  41.2 50.1 %copy-start.8 = (bf16[512,512]{1,0:T(8,128)(2,1)S(1)}, bf16[512,512]{1,0:T(8,128)(2,1)}, u32[]{:S(2)}) copy-start(bf16[512,512]{1,0:T(8,128)(2,1)} %get-tuple-element.16) | copy-start | bytes 1572868
  41.2 53.5 %copy-start.7 = (bf16[512,512]{1,0:T(8,128)(2,1)S(1)}, bf16[512,512]{1,0:T(8,128)(2,1)}, u32[]{:S(2)}) copy-start(bf16[512,512]{1,0:T(8,128)(2,1)} %get-tuple-element.17) | copy-start | bytes 1572868
  41.2 19.0 %all-to-all-start = ((bf16[8,32,640]{2,1,0:T(8,128)(2,1)}), bf16[8,32,640]{2,1,0:T(8,128)(2,1)S(1)}, u32[]{:S(2)}, u32[]{:S(2)}) async-start(bf16[8,32,640]{2,1,0:T(8,128)(2,1)} %bitcast.4), calls=%async_computation | async-start | bytes 655360 | tf_op jit(solution)/shard_map/all_to_all | solution.py:195
  60.2 14.8 %collective-permute-start.5 = (bf16[16,640]{1,0:T(8,128)(2,1)S(1)}, bf16[16,640]{1,0:T(8,128)(2,1)S(1)}, u32[]{:S(2)}, u32[]{:S(2)}) collective-permute-start(bf16[16,640]{1,0:T(8,128)(2,1)S(1)} %select_convert_fusion), channel_id=1, source_target_pairs={{0,53},{1,52},{2,51},{3,50},{4,49},{5,48},{48,5},{49,4},{50,3},{51... | collective-permute-start | bytes 61448 | tf_op jit(solution)/shard_map/ppermute | solution.py:21
  75.9 58.7 %all-to-all-start.1 = ((bf16[24,16,640]{2,1,0:T(8,128)(2,1)}), bf16[24,16,640]{2,1,0:T(8,128)(2,1)S(1)}, u32[]{:S(2)}, u32[]{:S(2)}) async-start(bf16[24,16,640]{2,1,0:T(8,128)(2,1)} %broadcast_in_dim.14), calls=%async_computation.1 | async-start | bytes 983040 | tf_op jit(solution)/shard_map/all_to_all | solution.py:202
  91.2 31.7 %collective-permute-start.2 = (bf16[512,512]{1,0:T(8,128)(2,1)S(1)}, bf16[512,512]{1,0:T(8,128)(2,1)S(1)}, u32[]{:S(2)}, u32[]{:S(2)}) collective-permute-start(bf16[512,512]{1,0:T(8,128)(2,1)S(1)} %copy-done.8), channel_id=1, source_target_pairs={{0,1},{1,2},{2,3},{3,4},{4,5},{5,6},{6,7},{7,8},{8,9},{9,10},{10,1... | collective-permute-start | bytes 1572872 | tf_op jit(solution)/shard_map/ppermute | solution.py:21
  94.6 35.8 %collective-permute-start.3 = (bf16[512,512]{1,0:T(8,128)(2,1)S(1)}, bf16[512,512]{1,0:T(8,128)(2,1)S(1)}, u32[]{:S(2)}, u32[]{:S(2)}) collective-permute-start(bf16[512,512]{1,0:T(8,128)(2,1)S(1)} %copy-done.7), channel_id=1, source_target_pairs={{0,767},{1,0},{2,1},{3,2},{4,3},{5,4},{6,5},{7,6},{8,7},{9,8},{10,... | collective-permute-start | bytes 1572872 | tf_op jit(solution)/shard_map/ppermute | solution.py:21
  122.9 7.5 %copy-start.1 = (bf16[512,512]{1,0:T(8,128)(2,1)}, bf16[512,512]{1,0:T(8,128)(2,1)S(1)}, u32[]{:S(2)}) copy-start(bf16[512,512]{1,0:T(8,128)(2,1)S(1)} %collective-permute-done.2.from_left) | copy-start | bytes 1572868
  130.4 0.8 copy-start.2

commit v2 on v1

--- a/solution.py
+++ b/solution.py
@@ -12,6 +12,7 @@
 SIZES = (8, 2, 2, 4, 6)
 NODE = AXES
 BITS = 5
+VMEM_LIMIT = 20 * 2**20
 f32 = jnp.float32
 bf16 = jnp.bfloat16
 
@@ -77,13 +78,14 @@
             jax.ShapeDtypeStruct((window, nodes), bf16),
         ],
         cost_estimate=pl.CostEstimate(flops=10**9, bytes_accessed=8 * 10**6, transcendentals=0),
+        compiler_params=pltpu.CompilerParams(vmem_limit_bytes=VMEM_LIMIT),
         name="adjacency",
     )(local_slot, neighbours, counts)
 
 
-def middle_kernel(
-    core_ref, adj, adjt, own, left, right, weight, bias, root, grad,
-    hidden, wsend, wkeep, part_left, part_right, part_own, agg_s, scaled_s, pre_s,
+def forward_kernel(
+    core_ref, adj, own, left, right, weight, bias, root, grad,
+    hidden, wsend, wkeep, scaled, agg_s, pre_s,
 ):
     nodes, width = own.shape
     rows = 128
@@ -99,11 +101,10 @@
         hidden[r, :] = (pre * gate).astype(bf16)
         grad_pre = grad[r, :].astype(f32) * gate * (1.0 + pre * (1.0 - gate))
         pre_s[r, :] = grad_pre.astype(bf16)
-        scaled_s[r, :] = (grad_pre * root[r, :]).astype(bf16)
-    scaled = scaled_s[...]
+        scaled[r, :] = (grad_pre * root[r, :]).astype(bf16)
     core = core_ref[0]
     ones = jnp.ones((nodes, 128), bf16)
-    wgrad = transposed_dot(agg_s[...], scaled).astype(bf16)
+    wgrad = transposed_dot(agg_s[...], scaled[...]).astype(bf16)
     bgrad = transposed_dot(pre_s[...], ones).astype(bf16)
     share = 16
     for chunk in range(width // share):
@@ -121,25 +122,52 @@
             wsend[place, 0:width] = wgrad[band]
             wsend[place, width : width + 128] = bgrad[band]
 
-    part_left[...] = rows_dot(adjt[0:nodes, :], scaled).astype(bf16)
-    part_right[...] = rows_dot(adjt[2 * nodes : 3 * nodes, :], scaled).astype(bf16)
-    part_own[...] = rows_dot(adjt[nodes : 2 * nodes, :], scaled)
-
-
-def middle(core, adj, adjt, own, left, right, weight, bias, root, grad):
+
+def forward(core, adj, own, left, right, weight, bias, root, grad):
     nodes, width = own.shape
     half = jax.ShapeDtypeStruct((width // 2, width + 128), bf16)
     square = jax.ShapeDtypeStruct((nodes, width), bf16)
     vmem = pl.BlockSpec(memory_space=pltpu.VMEM)
     return pl.pallas_call(
-        middle_kernel,
-        in_specs=[pl.BlockSpec(memory_space=pltpu.SMEM)] + [vmem] * 9,
-        out_specs=[vmem] * 6,
-        out_shape=[square, half, half, square, square, jax.ShapeDtypeStruct((nodes, width), f32)],
-        scratch_shapes=[pltpu.VMEM((nodes, width), bf16)] * 3,
-        cost_estimate=pl.CostEstimate(flops=2 * 10**9, bytes_accessed=10**7, transcendentals=0),
-        name="middle",
-    )(core, adj, adjt, own, left, right, weight, bias, root, grad)
+        forward_kernel,
+        in_specs=[pl.BlockSpec(memory_space=pltpu.SMEM)] + [vmem] * 8,
+        out_specs=[vmem] * 4,
+        out_shape=[square, half, half, square],
+        scratch_shapes=[pltpu.VMEM((nodes, width), bf16)] * 2,
+        compiler_params=pltpu.CompilerParams(vmem_limit_bytes=VMEM_LIMIT),
+        cost_estimate=pl.CostEstimate(flops=10**9, bytes_accessed=10**7, transcendentals=0),
+        name="forward",
+    )(core, adj, own, left, right, weight, bias, root, grad)
+
+
+def parts_kernel(adjt, scaled, part_left, part_right, part_own):
+    nodes = scaled.shape[0]
+    for first in range(0, nodes, 128):
+        r = pl.ds(first, 128)
+        part_left[r, :] = rows_dot(adjt[first : first + 128, :], scaled[...]).astype(bf16)
+    for first in range(0, nodes, 128):
+        r = pl.ds(first, 128)
+        low = 2 * nodes + first
+        part_right[r, :] = rows_dot(adjt[low : low + 128, :], scaled[...]).astype(bf16)
+    for first in range(0, nodes, 128):
+        r = pl.ds(first, 128)
+        low = nodes + first
+        part_own[r, :] = rows_dot(adjt[low : low + 128, :], scaled[...])
+
+
+def parts(adjt, scaled):
+    nodes, width = scaled.shape
+    square = jax.ShapeDtypeStruct((nodes, width), bf16)
+    vmem = pl.BlockSpec(memory_space=pltpu.VMEM)
+    return pl.pallas_call(
+        parts_kernel,
+        in_specs=[vmem] * 2,
+        out_specs=[vmem] * 3,
+        out_shape=[square, square, jax.ShapeDtypeStruct((nodes, width), f32)],
+        compiler_params=pltpu.CompilerParams(vmem_limit_bytes=VMEM_LIMIT),
+        cost_estimate=pl.CostEstimate(flops=10**9, bytes_accessed=10**7, transcendentals=0),
+        name="parts",
+    )(adjt, scaled)
 
 
 def final_kernel(part_own, from_left, from_right, root, weight, out):
@@ -162,6 +190,7 @@
         out_specs=vmem,
         out_shape=jax.ShapeDtypeStruct(part_own.shape, bf16),
         cost_estimate=pl.CostEstimate(flops=10**8, bytes_accessed=10**6, transcendentals=0),
+        compiler_params=pltpu.CompilerParams(vmem_limit_bytes=VMEM_LIMIT),
         name="final",
     )(part_own, from_left, from_right, root, weight)
 
@@ -181,10 +210,11 @@
     right = permute(own, NODE, lambda i: i - 1)
     adj, adjt = build_adjacency(local_slot, neighbours, counts)
     core = lax.axis_index("core").astype(jnp.int32).reshape(1)
-    hidden, wsend, wkeep, part_left, part_right, part_own = middle(
-        core, adj, adjt, own, left, right, weight, layer_bias[None, :], root, out_grad
+    hidden, wsend, wkeep, scaled = forward(
+        core, adj, own, left, right, weight, layer_bias[None, :], root, out_grad
     )
     got = permute(wsend, "core", lambda i: i ^ 1)
+    part_left, part_right, part_own = parts(adjt, scaled)
     from_right = permute(part_left, NODE, lambda i: i - 1)
     from_left = permute(part_right, NODE, lambda i: i + 1)
 
@@ -196,6 +226,7 @@
     high = lax.axis_index("zh")
     kept = jnp.where(high == 0, column[:share], column[share:])
     sent = jnp.where(high == 0, column[share:], column[:share]).astype(bf16)
+    sent, from_left, from_right = lax.optimization_barrier((sent, from_left, from_right))
     pair = kept + permute(sent, ("zh", "zl"), lambda i: -1 - i).astype(f32)
     spread = lax.axis_size(("x", "zl"))
     every = jnp.broadcast_to(pair.astype(bf16)[None], (spread, share, width + 128))

time: 137 us -> 128 us (0.934)
  the two profiles are of different devices: /device:TPU:128 before, /device:TPU:8 now
where the time goes in v2:
time: 128 us; the launch traced here: 127 us
  starting transfers between devices  56.9 us (44%)
  waiting for transfers between devices  46.5 us (36%)
  Pallas kernels  13.1 us (10%)
  local copies, waits for them, and re-layouts  5.92 us (5%)
  other arithmetic  3.93 us (3%)
    ppermute x6, starting transfers between devices, permute(): lax.ppermute(array, axes, [(i, route(i) % peers) for i in range(peers)])  39.3 us
    ppermute x6, waiting for transfers between devices, permute(): lax.ppermute(array, axes, [(i, route(i) % peers) for i in range(peers)])  28.6 us
    all_to_all x1, waiting for transfers between devices, local(): lax.all_to_all(every, ('x', 'zl'), 0, 0).astype(f32)  17.9 us
    all_to_all x1, starting transfers between devices, local(): lax.all_to_all(every, ('x', 'zl'), 0, 0).astype(f32)  8.83 us
    all_to_all x1, starting transfers between devices, local(): column = jnp.sum(lax.all_to_all(chip, 'y', 0, 0).astype(f32), axis=0)  8.76 us
    pallas_call x1, Pallas kernels, build_adjacency(): pl.pallas_call(adjacency_kernel, grid=(tiles,), in_specs=[pl.BlockSpec(me...  6.48 us
    unnamed x15, local copies, waits for them, and re-layouts  3.56 us
    pallas_call x1, Pallas kernels, forward(): pl.pallas_call(forward_kernel, in_specs=[pl.BlockSpec(memory_space=pltpu....  3.43 us
  transfers between devices with their start and end apart: 8, of which 6 were waited for; matrix products, arithmetic and copies ran while one was open for 2% of the time, Pallas kernels for 8%

profile of v2, /device:TPU:8, one launch (start us, length us, event | category | flops | bytes accessed | tf_op | source)
XLA Modules:
  0.0 127.2 jit_solution(996948777469048700)
XLA Ops:
  0.6 0.0 copy-start.5
  0.6 0.0 copy-start.6
  0.7 0.7 add_rsqrt_fusion
  1.4 1.2 multiply_convert_fusion.own
  2.6 16.1 %collective-permute-start.1 = (bf16[512,512]{1,0:T(8,128)(2,1)S(1)}, bf16[512,512]{1,0:T(8,128)(2,1)S(1)}, u32[]{:S(2)}, u32[]{:S(2)}) collective-permute-start(bf16[512,512]{1,0:T(8,128)(2,1)S(1)} %multiply_convert_fusion.own), channel_id=1, source_target_pairs={{0,767},{1,0},{2,1},{3,2},{4,3},{5,4},{6,5},{7,6},{8,7},{9,8},{10,... | collective-permute-start | bytes 1572872 | tf_op jit(solution)/shard_map/ppermute | solution.py:22
  18.7 1.9 %collective-permute-start = (bf16[512,512]{1,0:T(8,128)(2,1)S(1)}, bf16[512,512]{1,0:T(8,128)(2,1)S(1)}, u32[]{:S(2)}, u32[]{:S(2)}) collective-permute-start(bf16[512,512]{1,0:T(8,128)(2,1)S(1)} %multiply_convert_fusion.own), channel_id=1, source_target_pairs={{0,1},{1,2},{2,3},{3,4},{4,5},{5,6},{6,7},{7,8},{8,9},{9,10},{10,1... | collective-permute-start | bytes 1572872 | tf_op jit(solution)/shard_map/ppermute | solution.py:22
  20.7 0.1 copy.18.root
  20.8 1.0 copy.16.nbr_ref
  21.8 0.0 copy-done.5
  21.8 0.1 copy.17.cnt_ref
  22.0 0.0 copy-done.6
  22.0 0.0 copy-start
  22.0 0.0 copy-start.1
  22.0 0.0 copy-start.2
  22.1 6.5 %adjacency.1 = (bf16[512,1536]{1,0:T(8,128)(2,1)S(1)}, bf16[1536,512]{1,0:T(8,128)(2,1)S(1)}) custom-call(s32[4,6]{1,0:T(4,128)S(1)} %add_select_fusion.slot_ref, s32[512,30]{1,0:T(8,128)S(1)} %copy.16.nbr_ref, s32[512,1]{1,0:T(8,128)S(1)} %copy.17.cnt_ref), custom_call_target="tpu_custom_call" | custom-call | flops 1000000000 | bytes 8000000 | tf_op jit(solution)/shard_map/adjacency/pallas_call | solution.py:64
  28.5 0.0 copy-start.3
  28.6 1.1 copy-done.3
  29.7 0.0 collective-permute-done.1.right
  29.7 7.7 %collective-permute-done.left = bf16[512,512]{1,0:T(8,128)(2,1)S(1)} collective-permute-done((bf16[512,512]{1,0:T(8,128)(2,1)S(1)}, bf16[512,512]{1,0:T(8,128)(2,1)S(1)}, u32[]{:S(2)}, u32[]{:S(2)}) %collective-permute-start) | collective-permute-done | bytes 524320 | tf_op jit(solution)/shard_map/ppermute | solution.py:22
  37.4 0.0 copy-done
  37.4 0.0 copy-done.1
  37.5 0.0 copy-done.2
  37.5 3.4 %forward.1 = (bf16[512,512]{1,0:T(8,128)(2,1)}, bf16[256,640]{1,0:T(8,128)(2,1)S(1)}, bf16[256,640]{1,0:T(8,128)(2,1)S(1)}, bf16[512,512]{1,0:T(8,128)(2,1)S(1)}) custom-call(s32[1]{0:T(128)} %bitcast.core_ref, bf16[512,1536]{1,0:T(8,128)(2,1)S(1)} %get-tuple-element.16.adj, bf16[512,512]{1,0:T(8,128)(2,1)S(1)} %multiply_convert_fusion.own, ...), custom_call_target="tpu_custom_call" | custom-call | flops 1000000000 | bytes 10000000 | tf_op jit(solution)/shard_map/forward/pallas_call | solution.py:131
  40.9 3.3 %collective-permute-start.2 = (bf16[256,640]{1,0:T(8,128)(2,1)S(1)}, bf16[256,640]{1,0:T(8,128)(2,1)S(1)}, u32[]{:S(2)}, u32[]{:S(2)}) collective-permute-start(bf16[256,640]{1,0:T(8,128)(2,1)S(1)} %get-tuple-element.22), channel_id=1, source_target_pairs={{0,24},{24,0},{1,25},{25,1},{2,26},{26,2},{3,27},{27,3},{4,28},{28... | collective-permute-start | bytes 983048 | tf_op jit(solution)/shard_map/ppermute | solution.py:22
  44.2 1.2 collective-permute-done.2
  45.5 0.8 add_convert_fusion
  46.3 8.8 %all-to-all-start = ((bf16[8,32,640]{2,1,0:T(8,128)(2,1)}), bf16[8,32,640]{2,1,0:T(8,128)(2,1)}, u32[]{:S(2)}, u32[]{:S(2)}) async-start(bf16[8,32,640]{2,1,0:T(8,128)(2,1)} %bitcast.4), calls=%async_computation | async-start | bytes 655360 | tf_op jit(solution)/shard_map/all_to_all | solution.py:225
  55.1 0.0 copy-start.4
  55.1 1.4 %copy-done.4 = bf16[1536,512]{1,0:T(8,128)(2,1)S(1)} copy-done((bf16[1536,512]{1,0:T(8,128)(2,1)S(1)}, bf16[1536,512]{1,0:T(8,128)(2,1)}, u32[]{:S(2)}) %copy-start.4) | copy-done | bytes 1572888
  56.5 1.5 %parts.1 = (bf16[512,512]{1,0:T(8,128)(2,1)S(1)}, bf16[512,512]{1,0:T(8,128)(2,1)}, f32[512,512]{1,0:T(8,128)S(1)}) custom-call(bf16[1536,512]{1,0:T(8,128)(2,1)S(1)} %copy-done.4, bf16[512,512]{1,0:T(8,128)(2,1)S(1)} %get-tuple-element.19.scaled), custom_call_target="tpu_custom_call" | custom-call | flops 1000000000 | bytes 10000000 | tf_op jit(solution)/shard_map/parts/pallas_call | solution.py:162
  58.0 1.9 %collective-permute-start.3 = (bf16[512,512]{1,0:T(8,128)(2,1)}, bf16[512,512]{1,0:T(8,128)(2,1)S(1)}, u32[]{:S(2)}, u32[]{:S(2)}) collective-permute-start(bf16[512,512]{1,0:T(8,128)(2,1)} %get-tuple-element.23), channel_id=1, source_target_pairs={{0,1},{1,2},{2,3},{3,4},{4,5},{5,6},{6,7},{7,8},{8,9},{9,10},{10,1... | collective-permute-start | bytes 1572872 | tf_op jit(solution)/shard_map/ppermute | solution.py:22
  59.9 7.9 %collective-permute-start.4 = (bf16[512,512]{1,0:T(8,128)(2,1)S(1)}, bf16[512,512]{1,0:T(8,128)(2,1)S(1)}, u32[]{:S(2)}, u32[]{:S(2)}) collective-permute-start(bf16[512,512]{1,0:T(8,128)(2,1)S(1)} %get-tuple-element.24), channel_id=1, source_target_pairs={{0,767},{1,0},{2,1},{3,2},{4,3},{5,4},{6,5},{7,6},{8,7},{9,8},{10,... | collective-permute-start | bytes 1572872 | tf_op jit(solution)/shard_map/ppermute | solution.py:22
  67.8 0.0 all-to-all-done
  67.8 1.0 convert_reduce_fusion.1
  68.8 5.8 %collective-permute-done.3.from_left = bf16[512,512]{1,0:T(8,128)(2,1)S(1)} collective-permute-done((bf16[512,512]{1,0:T(8,128)(2,1)}, bf16[512,512]{1,0:T(8,128)(2,1)S(1)}, u32[]{:S(2)}, u32[]{:S(2)}) %collective-permute-start.3) | collective-permute-done | bytes 524320 | tf_op jit(solution)/shard_map/ppermute | solution.py:22
  74.6 12.1 %collective-permute-done.4.from_right = bf16[512,512]{1,0:T(8,128)(2,1)S(1)} collective-permute-done((bf16[512,512]{1,0:T(8,128)(2,1)S(1)}, bf16[512,512]{1,0:T(8,128)(2,1)S(1)}, u32[]{:S(2)}, u32[]{:S(2)}) %collective-permute-start.4) | collective-permute-done | bytes 524320 | tf_op jit(solution)/shard_map/ppermute | solution.py:22
  86.7 8.2 %collective-permute-start.5 = (bf16[16,640]{1,0:T(8,128)(2,1)S(1)}, bf16[16,640]{1,0:T(8,128)(2,1)S(1)}, u32[]{:S(2)}, u32[]{:S(2)}) collective-permute-start(bf16[16,640]{1,0:T(8,128)(2,1)S(1)} %select_convert_fusion), channel_id=1, source_target_pairs={{0,53},{1,52},{2,51},{3,50},{4,49},{5,48},{48,5},{49,4},{50,3},{51... | collective-permute-start | bytes 61448 | tf_op jit(solution)/shard_map/ppermute | solution.py:22
  94.8 1.8 %collective-permute-done.5 = bf16[16,640]{1,0:T(8,128)(2,1)S(1)} collective-permute-done((bf16[16,640]{1,0:T(8,128)(2,1)S(1)}, bf16[16,640]{1,0:T(8,128)(2,1)S(1)}, u32[]{:S(2)}, u32[]{:S(2)}) %collective-permute-start.5) | collective-permute-done | bytes 20512 | tf_op jit(solution)/shard_map/ppermute | solution.py:22
  96.7 0.8 broadcast_in_dim.14
  97.5 8.8 %all-to-all-start.1 = ((bf16[24,16,640]{2,1,0:T(8,128)(2,1)}), bf16[24,16,640]{2,1,0:T(8,128)(2,1)S(1)}, u32[]{:S(2)}, u32[]{:S(2)}) async-start(bf16[24,16,640]{2,1,0:T(8,128)(2,1)} %broadcast_in_dim.14), calls=%async_computation.1 | async-start | bytes 983040 | tf_op jit(solution)/shard_map/all_to_all | solution.py:233
  106.4 1.6 %final.1 = bf16[512,512]{1,0:T(8,128)(2,1)} custom-call(f32[512,512]{1,0:T(8,128)S(1)} %get-tuple-element.20.part_own, bf16[512,512]{1,0:T(8,128)(2,1)S(1)} %collective-permute-done.3.from_left, bf16[512,512]{1,0:T(8,128)(2,1)S(1)} %collective-permute-done.4.from_right, f32[512,1]{1,0:T(8,128)S(1)} %copy.18.root, bf16[512,512]{1,0:T(8,128)(2,1)S(1)} %copy-done), custom_call_target="tpu_custom_call" | custom-call | flops 100000000 | bytes 1000000 | tf_op jit(solution)/shard_map/final/pallas_call | solution.py:187
  108.0 17.9 %all-to-all-done.1 = bf16[24,16,640]{2,1,0:T(8,128)(2,1)S(1)} async-done(((bf16[24,16,640]{2,1,0:T(8,128)(2,1)}), bf16[24,16,640]{2,1,0:T(8,128)(2,1)S(1)}, u32[]{:S(2)}, u32[]{:S(2)}) %all-to-all-start.1) | async-done | bytes 491552 | tf_op jit(solution)/shard_map/all_to_all | solution.py:233
  125.9 0.1 convert_reduce_fusion
  125.9 0.6 slice_reduce_fusion
  126.6 0.6 slice.20
  (4 shorter events, 0.0 us)
Async XLA Ops:
  0.6 21.2 %copy-start.5 = (s32[512]{0:T(512)S(1)}, s32[512]{0:T(512)}, u32[]{:S(2)}) copy-start(s32[512]{0:T(512)} %param.12) | copy-start | bytes 6148
  0.6 21.4 %copy-start.6 = (s32[4,6]{1,0:T(4,128)S(1)}, s32[4,6]{1,0:T(4,128)}, u32[]{:S(2)}) copy-start(s32[4,6]{1,0:T(4,128)} %param.10) | copy-start | bytes 292
  2.6 27.1 %collective-permute-start.1 = (bf16[512,512]{1,0:T(8,128)(2,1)S(1)}, bf16[512,512]{1,0:T(8,128)(2,1)S(1)}, u32[]{:S(2)}, u32[]{:S(2)}) collective-permute-start(bf16[512,512]{1,0:T(8,128)(2,1)S(1)} %multiply_convert_fusion.own), channel_id=1, source_target_pairs={{0,767},{1,0},{2,1},{3,2},{4,3},{5,4},{6,5},{7,6},{8,7},{9,8},{10,... | collective-permute-start | bytes 1572872 | tf_op jit(solution)/shard_map/ppermute | solution.py:22
  18.7 18.7 %collective-permute-start = (bf16[512,512]{1,0:T(8,128)(2,1)S(1)}, bf16[512,512]{1,0:T(8,128)(2,1)S(1)}, u32[]{:S(2)}, u32[]{:S(2)}) collective-permute-start(bf16[512,512]{1,0:T(8,128)(2,1)S(1)} %multiply_convert_fusion.own), channel_id=1, source_target_pairs={{0,1},{1,2},{2,3},{3,4},{4,5},{5,6},{6,7},{7,8},{8,9},{9,10},{10,1... | collective-permute-start | bytes 1572872 | tf_op jit(solution)/shard_map/ppermute | solution.py:22
  22.0 15.4 %copy-start = (bf16[512,512]{1,0:T(8,128)(2,1)S(1)}, bf16[512,512]{1,0:T(8,128)(2,1)}, u32[]{:S(2)}) copy-start(bf16[512,512]{1,0:T(8,128)(2,1)} %weight.3) | copy-start | bytes 1572868
  22.0 15.4 %copy-start.1 = (bf16[512,512]{1,0:T(8,128)(2,1)S(1)}, bf16[512,512]{1,0:T(8,128)(2,1)}, u32[]{:S(2)}) copy-start(bf16[512,512]{1,0:T(8,128)(2,1)} %grad.1) | copy-start | bytes 1572868
  22.0 15.4 %copy-start.2 = (f32[512]{0:T(512)S(1)}, f32[512]{0:T(512)}, u32[]{:S(2)}) copy-start(f32[512]{0:T(512)} %param.9) | copy-start | bytes 6148
  28.5 1.2 copy-start.3
  40.9 4.6 %collective-permute-start.2 = (bf16[256,640]{1,0:T(8,128)(2,1)S(1)}, bf16[256,640]{1,0:T(8,128)(2,1)S(1)}, u32[]{:S(2)}, u32[]{:S(2)}) collective-permute-start(bf16[256,640]{1,0:T(8,128)(2,1)S(1)} %get-tuple-element.22), channel_id=1, source_target_pairs={{0,24},{24,0},{1,25},{25,1},{2,26},{26,2},{3,27},{27,3},{4,28},{28... | collective-permute-start | bytes 983048 | tf_op jit(solution)/shard_map/ppermute | solution.py:22
  46.3 21.5 %all-to-all-start = ((bf16[8,32,640]{2,1,0:T(8,128)(2,1)}), bf16[8,32,640]{2,1,0:T(8,128)(2,1)}, u32[]{:S(2)}, u32[]{:S(2)}) async-start(bf16[8,32,640]{2,1,0:T(8,128)(2,1)} %bitcast.4), calls=%async_computation | async-start | bytes 655360 | tf_op jit(solution)/shard_map/all_to_all | solution.py:225
  55.1 1.4 %copy-start.4 = (bf16[1536,512]{1,0:T(8,128)(2,1)S(1)}, bf16[1536,512]{1,0:T(8,128)(2,1)}, u32[]{:S(2)}) copy-start(bf16[1536,512]{1,0:T(8,128)(2,1)} %copy-done.3) | copy-start | bytes 4718596
  58.0 16.6 %collective-permute-start.3 = (bf16[512,512]{1,0:T(8,128)(2,1)}, bf16[512,512]{1,0:T(8,128)(2,1)S(1)}, u32[]{:S(2)}, u32[]{:S(2)}) collective-permute-start(bf16[512,512]{1,0:T(8,128)(2,1)} %get-tuple-element.23), channel_id=1, source_target_pairs={{0,1},{1,2},{2,3},{3,4},{4,5},{5,6},{6,7},{7,8},{8,9},{9,10},{10,1... | collective-permute-start | bytes 1572872 | tf_op jit(solution)/shard_map/ppermute | solution.py:22
  59.9 26.8 %collective-permute-start.4 = (bf16[512,512]{1,0:T(8,128)(2,1)S(1)}, bf16[512,512]{1,0:T(8,128)(2,1)S(1)}, u32[]{:S(2)}, u32[]{:S(2)}) collective-permute-start(bf16[512,512]{1,0:T(8,128)(2,1)S(1)} %get-tuple-element.24), channel_id=1, source_target_pairs={{0,767},{1,0},{2,1},{3,2},{4,3},{5,4},{6,5},{7,6},{8,7},{9,8},{10,... | collective-permute-start | bytes 1572872 | tf_op jit(solution)/shard_map/ppermute | solution.py:22
  86.7 10.0 %collective-permute-start.5 = (bf16[16,640]{1,0:T(8,128)(2,1)S(1)}, bf16[16,640]{1,0:T(8,128)(2,1)S(1)}, u32[]{:S(2)}, u32[]{:S(2)}) collective-permute-start(bf16[16,640]{1,0:T(8,128)(2,1)S(1)} %select_convert_fusion), channel_id=1, source_target_pairs={{0,53},{1,52},{2,51},{3,50},{4,49},{5,48},{48,5},{49,4},{50,3},{51... | collective-permute-start | bytes 61448 | tf_op jit(solution)/shard_map/ppermute | solution.py:22
  97.5 28.3 %all-to-all-start.1 = ((bf16[24,16,640]{2,1,0:T(8,128)(2,1)}), bf16[24,16,640]{2,1,0:T(8,128)(2,1)S(1)}, u32[]{:S(2)}, u32[]{:S(2)}) async-start(bf16[24,16,640]{2,1,0:T(8,128)(2,1)} %broadcast_in_dim.14), calls=%async_computation.1 | async-start | bytes 983040 | tf_op jit(solution)/shard_map/all_to_all | solution.py:233

commit v3 on v2

v3 whole, which is shorter than its diff:
```python
import math

import jax
import jax.numpy as jnp
from jax import lax
from jax.experimental import pallas as pl
from jax.experimental.pallas import tpu as pltpu
from jax.sharding import Mesh
from jax.sharding import PartitionSpec as P

AXES = ("y", "zh", "core", "x", "zl")
SIZES = (8, 2, 2, 4, 6)
NODE = AXES
BITS = 5
VMEM_LIMIT = 20 * 2**20
f32 = jnp.float32
bf16 = jnp.bfloat16


def permute(array, axes, route):
    peers = lax.axis_size(axes)
    return lax.ppermute(array, axes, [(i, route(i) % peers) for i in range(peers)])


def near_partner(i):
    return i ^ 1


def far_partner(i):
    return i + 1 if i % 2 else i - 1


def rows_dot(a, b):
    return jnp.dot(a, b, preferred_element_type=f32)


def transposed_dot(a, b):
    return lax.dot_general(a, b, (((0,), (0,)), ((), ())), preferred_element_type=f32)


def adjacency_kernel(slot_ref, nbr_ref, cnt_ref, adj_ref, edge_ref, own_ref):
    tile = pl.program_id(0)
    rows, width = nbr_ref.shape
    slots = slot_ref.shape[1]
    tiles = adj_ref.shape[1] // rows
    own_first = tiles // 3
    nbr = nbr_ref[...]
    live = lax.broadcasted_iota(jnp.int32, nbr.shape, 1) < cnt_ref[...]
    low = jnp.bitwise_and(nbr, rows - 1)
    shift = BITS * lax.shift_right_logical(nbr, rows.bit_length() - 1)
    step = jnp.where(live, lax.shift_left(jnp.ones_like(nbr), shift), 0)
    lane = lax.broadcasted_iota(jnp.int32, (rows, rows), 1)
    packed = jnp.zeros((rows, rows), jnp.int32)
    for k in range(width):
        packed += jnp.where(lane == low[:, k : k + 1], step[:, k : k + 1], 0)
    adj_ref[...] = jnp.zeros_like(adj_ref)
    row = lax.broadcasted_iota(jnp.int32, (rows, rows), 0)
    own = pl.ds(pl.multiple_of((own_first + tile) * rows, rows), rows)
    adj_ref[:, own] = (row == lane).astype(f32).astype(bf16)
    for s in range(slots):
        counts = jnp.bitwise_and(lax.shift_right_logical(packed, BITS * s), 2**BITS - 1)
        place = pl.ds(pl.multiple_of(slot_ref[tile, s] * rows, rows), rows)
        adj_ref[:, place] += counts.astype(f32).astype(bf16)
    nodes = tiles // 3 * rows
    edge_ref[0:nodes, :] = adj_ref[:, 0:nodes].T
    edge_ref[nodes : 2 * nodes, :] = adj_ref[:, 2 * nodes : 3 * nodes].T
    own_ref[...] = adj_ref[:, nodes : 2 * nodes].T


def build_adjacency(local_slot, neighbours, counts):
    tiles, slots = local_slot.shape
    nodes, width = neighbours.shape
    rows = nodes // tiles
    window = 3 * nodes
    return pl.pallas_call(
        adjacency_kernel,
        grid=(tiles,),
        in_specs=[
            pl.BlockSpec(memory_space=pltpu.SMEM),
            pl.BlockSpec((rows, width), lambda t: (t, 0)),
            pl.BlockSpec((rows, 1), lambda t: (t, 0)),
        ],
        out_specs=[
            pl.BlockSpec((rows, window), lambda t: (t, 0)),
            pl.BlockSpec((2 * nodes, rows), lambda t: (0, t)),
            pl.BlockSpec((nodes, rows), lambda t: (0, t)),
        ],
        out_shape=[
            jax.ShapeDtypeStruct((nodes, window), bf16),
            jax.ShapeDtypeStruct((2 * nodes, nodes), bf16),
            jax.ShapeDtypeStruct((nodes, nodes), bf16),
        ],
        cost_estimate=pl.CostEstimate(flops=10**9, bytes_accessed=8 * 10**6, transcendentals=0),
        compiler_params=pltpu.CompilerParams(vmem_limit_bytes=VMEM_LIMIT),
        name="adjacency",
    )(local_slot, neighbours, counts)


def forward_kernel(
    core_ref, adj, own, near, far, weight, bias, root, grad,
    hidden, wsend, wkeep, scaled, agg_s, pre_s,
):
    nodes, width = own.shape
    rows = 128
    for first in range(0, nodes, rows):
        r = pl.ds(first, rows)
        agg = rows_dot(adj[r, 0:nodes], near[...])
        agg += rows_dot(adj[r, nodes : 2 * nodes], own[...])
        agg += rows_dot(adj[r, 2 * nodes : 3 * nodes], far[...])
        agg = agg.astype(bf16)
        agg_s[r, :] = agg
        pre = root[r, :] * rows_dot(agg, weight[...]) + bias[...]
        gate = jax.nn.sigmoid(pre)
        hidden[r, :] = (pre * gate).astype(bf16)
        grad_pre = grad[r, :].astype(f32) * gate * (1.0 + pre * (1.0 - gate))
        pre_s[r, :] = grad_pre.astype(bf16)
        scaled[r, :] = (grad_pre * root[r, :]).astype(bf16)
    core = core_ref[0]
    ones = jnp.ones((nodes, 128), bf16)
    wgrad = transposed_dot(agg_s[...], scaled[...]).astype(bf16)
    bgrad = transposed_dot(pre_s[...], ones).astype(bf16)
    share = 16
    for chunk in range(width // share):
        outer, side = divmod(chunk, 2)
        band = slice(chunk * share, (chunk + 1) * share)
        place = pl.ds(outer * share, share)

        @pl.when(core == side)
        def _():
            wkeep[place, 0:width] = wgrad[band]
            wkeep[place, width : width + 128] = bgrad[band]

        @pl.when(core != side)
        def _():
            wsend[place, 0:width] = wgrad[band]
            wsend[place, width : width + 128] = bgrad[band]


def forward(core, adj, own, near, far, weight, bias, root, grad):
    nodes, width = own.shape
    half = jax.ShapeDtypeStruct((width // 2, width + 128), bf16)
    square = jax.ShapeDtypeStruct((nodes, width), bf16)
    vmem = pl.BlockSpec(memory_space=pltpu.VMEM)
    return pl.pallas_call(
        forward_kernel,
        in_specs=[pl.BlockSpec(memory_space=pltpu.SMEM)] + [vmem] * 8,
        out_specs=[vmem] * 4,
        out_shape=[square, half, half, square],
        scratch_shapes=[pltpu.VMEM((nodes, width), bf16)] * 2,
        compiler_params=pltpu.CompilerParams(vmem_limit_bytes=VMEM_LIMIT),
        cost_estimate=pl.CostEstimate(flops=10**9, bytes_accessed=10**7, transcendentals=0),
        name="forward",
    )(core, adj, own, near, far, weight, bias, root, grad)


def parts_kernel(edge, scaled, part_near, part_far):
    nodes = scaled.shape[0]
    rows = 128
    for first in range(0, nodes, rows):
        part = rows_dot(edge[first : first + rows, :], scaled[...])
        part_near[first : first + rows, :] = part.astype(bf16)
        part = rows_dot(edge[nodes + first : nodes + first + rows, :], scaled[...])
        part_far[first : first + rows, :] = part.astype(bf16)


def parts(edge, scaled):
    square = jax.ShapeDtypeStruct(scaled.shape, bf16)
    vmem = pl.BlockSpec(memory_space=pltpu.VMEM)
    return pl.pallas_call(
        parts_kernel,
        in_specs=[vmem] * 2,
        out_specs=[vmem] * 2,
        out_shape=[square, square],
        compiler_params=pltpu.CompilerParams(vmem_limit_bytes=VMEM_LIMIT),
        cost_estimate=pl.CostEstimate(flops=10**8, bytes_accessed=10**6, transcendentals=0),
        name="parts",
    )(edge, scaled)


def spread_kernel(blocks, out):
    count = blocks.shape[0]
    total = blocks[0].astype(f32)
    for i in range(1, count):
        total += blocks[i].astype(f32)
    total = total.astype(bf16)
    copies, rows = out.shape[0], out.shape[1]
    each = copies * rows // blocks.shape[1]
    for i in range(copies):
        first = i // each * rows
        out[i] = total[first : first + rows]


def spread(blocks, pieces, copies):
    _, rows, width = blocks.shape
    vmem = pl.BlockSpec(memory_space=pltpu.VMEM)
    return pl.pallas_call(
        spread_kernel,
        in_specs=[vmem],
        out_specs=vmem,
        out_shape=jax.ShapeDtypeStruct((pieces * copies, rows // pieces, width), bf16),
        compiler_params=pltpu.CompilerParams(vmem_limit_bytes=VMEM_LIMIT),
        cost_estimate=pl.CostEstimate(flops=10**6, bytes_accessed=10**6, transcendentals=0),
        name="spread",
    )(blocks)


def last_sum_kernel(scale, blocks, out, bias):
    count, rows, width = blocks.shape
    total = blocks[0].astype(f32)
    for i in range(1, count):
        total += blocks[i].astype(f32)
    total = total * scale
    wide = out.shape[1]
    out[...] = total[:, 0:wide]
    column = total[:, wide:width]
    row = lax.broadcasted_iota(jnp.int32, column.shape, 0)
    lane = lax.broadcasted_iota(jnp.int32, column.shape, 1)
    flat = jnp.sum(jnp.where(row == lane, column, 0.0), axis=0, keepdims=True)
    bias[...] = flat[:, 0:rows]


def last_sum(blocks, scale):
    _, rows, width = blocks.shape
    vmem = pl.BlockSpec(memory_space=pltpu.VMEM)
    return pl.pallas_call(
        lambda *refs: last_sum_kernel(scale, *refs),
        in_specs=[vmem],
        out_specs=[vmem] * 2,
        out_shape=[
            jax.ShapeDtypeStruct((rows, width - 128), f32),
            jax.ShapeDtypeStruct((1, rows), f32),
        ],
        compiler_params=pltpu.CompilerParams(vmem_limit_bytes=VMEM_LIMIT),
        cost_estimate=pl.CostEstimate(flops=10**6, bytes_accessed=10**6, transcendentals=0),
        name="last_sum",
    )(blocks)


def own_part_kernel(adj, scaled, out):
    rows = 128
    for first in range(0, out.shape[0], rows):
        out[first : first + rows, :] = rows_dot(adj[first : first + rows, :], scaled[...])


def own_part(adj, scaled):
    vmem = pl.BlockSpec(memory_space=pltpu.VMEM)
    return pl.pallas_call(
        own_part_kernel,
        in_specs=[vmem] * 2,
        out_specs=vmem,
        out_shape=jax.ShapeDtypeStruct(scaled.shape, f32),
        compiler_params=pltpu.CompilerParams(vmem_limit_bytes=VMEM_LIMIT),
        cost_estimate=pl.CostEstimate(flops=10**12, bytes_accessed=10**9, transcendentals=0),
        name="own_part",
    )(adj, scaled)


def final_kernel(part_own, from_near, from_far, root, weight, out):
    nodes = out.shape[0]
    rows = 128
    for first in range(0, nodes, rows):
        r = pl.ds(first, rows)
        total = part_own[r, :] + from_near[r, :].astype(f32) + from_far[r, :].astype(f32)
        grad_proj = (root[r, :] * total).astype(bf16)
        out[r, :] = lax.dot_general(
            grad_proj, weight[...], (((1,), (1,)), ((), ())), preferred_element_type=f32
        ).astype(bf16)


def final(part_own, from_near, from_far, root, weight):
    vmem = pl.BlockSpec(memory_space=pltpu.VMEM)
    return pl.pallas_call(
        final_kernel,
        in_specs=[vmem] * 5,
        out_specs=vmem,
        out_shape=jax.ShapeDtypeStruct(part_own.shape, bf16),
        cost_estimate=pl.CostEstimate(flops=10**8, bytes_accessed=10**6, transcendentals=0),
        compiler_params=pltpu.CompilerParams(vmem_limit_bytes=VMEM_LIMIT),
        name="final",
    )(part_own, from_near, from_far, root, weight)


def local(features, weight, layer_bias, block_cols, neighbours, row_counts, out_grad):
    nodes, width = features.shape
    tile_count = block_cols.shape[0]
    devices = lax.axis_size(NODE)
    all_tiles = tile_count * devices
    normaliser = 1.0 / math.sqrt(nodes * devices)
    window_start = (lax.axis_index(NODE) - 1) * tile_count
    local_slot = jnp.mod(block_cols - window_start, all_tiles)
    group = local_slot // tile_count
    even = lax.axis_index(NODE) % 2 == 0
    local_slot = jnp.where(even, local_slot + 2 * (1 - group) * tile_count, local_slot)
    counts = row_counts[:, None]
    root = lax.rsqrt(1.0 + counts.astype(f32))
    own = (features.astype(f32) * root).astype(bf16)
    far = permute(own, NODE, far_partner)
    near = permute(own, NODE, near_partner)
    adj, edge, own_t = build_adjacency(local_slot, neighbours, counts)
    core = lax.axis_index("core").astype(jnp.int32).reshape(1)
    hidden, wsend, wkeep, scaled = forward(
        core, adj, own, near, far, weight, layer_bias[None, :], root, out_grad
    )
    got = permute(wsend, "core", lambda i: i ^ 1)
    part_near, part_far = parts(edge, scaled)
    from_far = permute(part_far, NODE, far_partner)
    from_near = permute(part_near, NODE, near_partner)
    ny, nx, nzh, nzl = (lax.axis_size(n) for n in ("y", "x", "zh", "zl"))
    chip = (wkeep.astype(f32) + got.astype(f32)).astype(bf16)
    blocks = lax.all_to_all(chip.reshape(ny, -1, width + 128), "y", 0, 0)
    blocks = lax.all_to_all(spread(blocks, nzh, nzl), ("zh", "zl"), 0, 0)
    part_own = own_part(own_t, scaled)
    blocks, part_own = lax.optimization_barrier((blocks, part_own))
    blocks = spread(blocks, 1, nx)
    blocks, from_near, from_far = lax.optimization_barrier((blocks, from_near, from_far))
    blocks = lax.all_to_all(blocks, "x", 0, 0)
    weight_grad, bias_grad = last_sum(blocks, normaliser)
    input_grad = final(part_own, from_near, from_far, root, weight)
    return (hidden, input_grad, weight_grad, bias_grad[0])


def solution(mesh):
    wide = Mesh(mesh.devices.reshape(SIZES), AXES)
    row = P(NODE, None)
    in_specs = (row, P(), P(), row, row, P(NODE), row)
    shares = ("y", "zh", "core")
    out_specs = (row, row, P(shares, None), P(shares))
    return jax.shard_map(local, mesh=wide, in_specs=in_specs, out_specs=out_specs, check_vma=False)
```

time: 128 us -> 114 us (0.89)
  waiting for transfers between devices: 46.5 us -> 32.1 us
  Pallas kernels: 13.1 us -> 17.8 us
  local copies, waits for them, and re-layouts: 5.92 us -> 1.31 us
    ppermute x6 -> x5, waiting for transfers between devices: 28.6 us -> 11.8 us  [permute(): lax.ppermute(array, axes, [(i, route(i) % peers) for i in range(peers)])]
    all_to_all x2 -> x3, starting transfers between devices: 17.6 us -> 28 us  [the longest x1 10.8 us: local(): blocks = lax.all_to_all(blocks, 'x', 0, 0)]
    ppermute x6 -> x5, starting transfers between devices: 39.3 us -> 30.1 us  [permute(): lax.ppermute(array, axes, [(i, route(i) % peers) for i in range(peers)])]
    pallas_call x1 -> x5, Pallas kernels: 1.51 us -> 5.07 us  [the longest x2 2.35 us: spread(): pl.pallas_call(spread_kernel, in_specs=[vmem], out_specs=vmem, out_shape=...]
    unnamed x15 -> x17, local copies, waits for them, and re-layouts: 3.56 us -> 1.02 us
    all_to_all x2 -> x3, waiting for transfers between devices: 17.9 us -> 20.4 us  [the longest x1 17.2 us: local(): blocks = lax.all_to_all(spread(blocks, nzh, nzl), ('zh', 'zl'), 0, 0)]
  transfers between devices with their start and end apart: 8 -> 8, of which waited for: 6 -> 6; matrix products, arithmetic and copies ran while one was open for 2% -> 1% of each run, Pallas kernels for 8% -> 12%
where the time goes in v3:
time: 114 us; the launch traced here: 113 us
  starting transfers between devices  58.1 us (51%)
  waiting for transfers between devices  32.1 us (28%)
  Pallas kernels  17.8 us (16%)
  other arithmetic  2.79 us (2%)
  local copies, waits for them, and re-layouts  1.31 us (1%)
    ppermute x5, starting transfers between devices, permute(): lax.ppermute(array, axes, [(i, route(i) % peers) for i in range(peers)])  30.1 us
    all_to_all x1, waiting for transfers between devices, local(): blocks = lax.all_to_all(spread(blocks, nzh, nzl), ('zh', 'zl'), 0, 0)  17.2 us
    ppermute x5, waiting for transfers between devices, permute(): lax.ppermute(array, axes, [(i, route(i) % peers) for i in range(peers)])  11.8 us
    all_to_all x1, starting transfers between devices, local(): blocks = lax.all_to_all(blocks, 'x', 0, 0)  10.8 us
    all_to_all x1, starting transfers between devices, local(): blocks = lax.all_to_all(spread(blocks, nzh, nzl), ('zh', 'zl'), 0, 0)  9.49 us
    all_to_all x1, starting transfers between devices, local(): blocks = lax.all_to_all(chip.reshape(ny, -1, width + 128), 'y', 0, 0)  7.67 us
    pallas_call x1, Pallas kernels, build_adjacency(): pl.pallas_call(adjacency_kernel, grid=(tiles,), in_specs=[pl.BlockSpec(me...  6.48 us
    pallas_call x1, Pallas kernels, forward(): pl.pallas_call(forward_kernel, in_specs=[pl.BlockSpec(memory_space=pltpu....  3.46 us
  transfers between devices with their start and end apart: 8, of which 6 were waited for; matrix products, arithmetic and copies ran while one was open for 1% of the time, Pallas kernels for 12%

profile of v3, /device:TPU:8, one launch (start us, length us, event | category | flops | bytes accessed | tf_op | source)
XLA Modules:
  0.0 113.0 jit_solution(11231709721756837439)
XLA Ops:
  0.6 0.0 copy-start.6
  0.6 0.0 copy-start.7
  0.7 0.7 add_rsqrt_fusion
  1.4 1.2 %multiply_convert_fusion.own = bf16[512,512]{1,0:T(8,128)(2,1)S(1)} fusion(bf16[512,512]{1,0:T(8,128)(2,1)} %param.7, f32[512]{0:T(512)S(1)} %add_rsqrt_fusion), kind=kLoop, calls=%fused_computation | loop fusion | flops 786432 | bytes 1050624 | tf_op jit(solution)/shard_map/convert_element_type | solution.py:296
  2.6 16.1 %collective-permute-start.1 = (bf16[512,512]{1,0:T(8,128)(2,1)S(1)}, bf16[512,512]{1,0:T(8,128)(2,1)S(1)}, u32[]{:S(2)}, u32[]{:S(2)}) collective-permute-start(bf16[512,512]{1,0:T(8,128)(2,1)S(1)} %multiply_convert_fusion.own), channel_id=1, source_target_pairs={{0,767},{1,2},{2,1},{3,4},{4,3},{5,6},{6,5},{7,8},{8,7},{9,10},{10... | collective-permute-start | bytes 1572872 | tf_op jit(solution)/shard_map/ppermute | solution.py:22
  18.7 1.9 %collective-permute-start = (bf16[512,512]{1,0:T(8,128)(2,1)S(1)}, bf16[512,512]{1,0:T(8,128)(2,1)S(1)}, u32[]{:S(2)}, u32[]{:S(2)}) collective-permute-start(bf16[512,512]{1,0:T(8,128)(2,1)S(1)} %multiply_convert_fusion.own), channel_id=1, source_target_pairs={{0,1},{1,0},{2,3},{3,2},{4,5},{5,4},{6,7},{7,6},{8,9},{9,8},{10,11... | collective-permute-start | bytes 1572872 | tf_op jit(solution)/shard_map/ppermute | solution.py:22
  20.7 0.1 copy.14.root
  20.8 1.0 copy.12.nbr_ref
  21.8 0.0 copy-done.6
  21.8 0.1 copy.13.cnt_ref
  22.0 0.0 copy-done.7
  22.0 0.0 copy-start
  22.0 0.0 copy-start.2
  22.1 0.0 copy-start.3
  22.1 6.5 %adjacency.1 = (bf16[512,1536]{1,0:T(8,128)(2,1)S(1)}, bf16[1024,512]{1,0:T(8,128)(2,1)S(1)}, bf16[512,512]{1,0:T(8,128)(2,1)S(1)}) custom-call(s32[4,6]{1,0:T(4,128)S(1)} %add_select_fusion.slot_ref, s32[512,30]{1,0:T(8,128)S(1)} %copy.12.nbr_ref, s32[512,1]{1,0:T(8,128)S(1)} %copy.13.cnt_ref), custom_call_target="tpu_custom_call" | custom-call | flops 1000000000 | bytes 8000000 | tf_op jit(solution)/shard_map/adjacency/pallas_call | solution.py:75
  28.6 0.0 copy-start.4
  28.6 1.9 %collective-permute-done.1.far = bf16[512,512]{1,0:T(8,128)(2,1)S(1)} collective-permute-done((bf16[512,512]{1,0:T(8,128)(2,1)S(1)}, bf16[512,512]{1,0:T(8,128)(2,1)S(1)}, u32[]{:S(2)}, u32[]{:S(2)}) %collective-permute-start.1) | collective-permute-done | bytes 524320 | tf_op jit(solution)/shard_map/ppermute | solution.py:22
  30.5 8.3 %collective-permute-done.near = bf16[512,512]{1,0:T(8,128)(2,1)S(1)} collective-permute-done((bf16[512,512]{1,0:T(8,128)(2,1)S(1)}, bf16[512,512]{1,0:T(8,128)(2,1)S(1)}, u32[]{:S(2)}, u32[]{:S(2)}) %collective-permute-start) | collective-permute-done | bytes 524320 | tf_op jit(solution)/shard_map/ppermute | solution.py:22
  38.7 0.0 copy-done
  38.7 0.0 copy-done.2
  38.7 0.0 copy-done.3
  38.7 3.5 %forward.1 = (bf16[512,512]{1,0:T(8,128)(2,1)}, bf16[256,640]{1,0:T(8,128)(2,1)S(1)}, bf16[256,640]{1,0:T(8,128)(2,1)S(1)}, bf16[512,512]{1,0:T(8,128)(2,1)S(1)}) custom-call(s32[1]{0:T(128)} %bitcast.core_ref, bf16[512,1536]{1,0:T(8,128)(2,1)S(1)} %get-tuple-element.20.adj, bf16[512,512]{1,0:T(8,128)(2,1)S(1)} %multiply_convert_fusion.own, ...), custom_call_target="tpu_custom_call" | custom-call | flops 1000000000 | bytes 10000000 | tf_op jit(solution)/shard_map/forward/pallas_call | solution.py:144
  42.2 0.0 copy-done.4
  42.2 1.9 %collective-permute-start.2 = (bf16[256,640]{1,0:T(8,128)(2,1)S(1)}, bf16[256,640]{1,0:T(8,128)(2,1)S(1)}, u32[]{:S(2)}, u32[]{:S(2)}) collective-permute-start(bf16[256,640]{1,0:T(8,128)(2,1)S(1)} %get-tuple-element.23), channel_id=1, source_target_pairs={{0,24},{24,0},{1,25},{25,1},{2,26},{26,2},{3,27},{27,3},{4,28},{28... | collective-permute-start | bytes 983048 | tf_op jit(solution)/shard_map/ppermute | solution.py:22
  44.1 1.6 %collective-permute-done.2 = bf16[256,640]{1,0:T(8,128)(2,1)S(1)} collective-permute-done((bf16[256,640]{1,0:T(8,128)(2,1)S(1)}, bf16[256,640]{1,0:T(8,128)(2,1)S(1)}, u32[]{:S(2)}, u32[]{:S(2)}) %collective-permute-start.2) | collective-permute-done | bytes 327712 | tf_op jit(solution)/shard_map/ppermute | solution.py:22
  45.7 0.8 add_convert_fusion
  46.5 0.0 copy-start.5
  46.5 7.7 %all-to-all-start = ((bf16[8,32,640]{2,1,0:T(8,128)(2,1)}), bf16[8,32,640]{2,1,0:T(8,128)(2,1)S(1)}, u32[]{:S(2)}, u32[]{:S(2)}) async-start(bf16[8,32,640]{2,1,0:T(8,128)(2,1)} %bitcast.4), calls=%async_computation | async-start | bytes 655360 | tf_op jit(solution)/shard_map/all_to_all | solution.py:310
  54.2 1.7 %parts.1 = (bf16[512,512]{1,0:T(8,128)(2,1)}, bf16[512,512]{1,0:T(8,128)(2,1)}) custom-call(bf16[1024,512]{1,0:T(8,128)(2,1)S(1)} %get-tuple-element.28.edge, bf16[512,512]{1,0:T(8,128)(2,1)S(1)} %get-tuple-element.25.scaled), custom_call_target="tpu_custom_call" | custom-call | flops 100000000 | bytes 1000000 | tf_op jit(solution)/shard_map/parts/pallas_call | solution.py:169
  55.9 1.9 %collective-permute-start.3 = (bf16[512,512]{1,0:T(8,128)(2,1)}, bf16[512,512]{1,0:T(8,128)(2,1)}, u32[]{:S(2)}, u32[]{:S(2)}) collective-permute-start(bf16[512,512]{1,0:T(8,128)(2,1)} %get-tuple-element.29), channel_id=1, source_target_pairs={{0,1},{1,0},{2,3},{3,2},{4,5},{5,4},{6,7},{7,6},{8,9},{9,8},{10,11... | collective-permute-start | bytes 1572872 | tf_op jit(solution)/shard_map/ppermute | solution.py:22
  57.8 8.3 %collective-permute-start.4 = (bf16[512,512]{1,0:T(8,128)(2,1)}, bf16[512,512]{1,0:T(8,128)(2,1)}, u32[]{:S(2)}, u32[]{:S(2)}) collective-permute-start(bf16[512,512]{1,0:T(8,128)(2,1)} %get-tuple-element.30), channel_id=1, source_target_pairs={{0,767},{1,2},{2,1},{3,4},{4,3},{5,6},{6,5},{7,8},{8,7},{9,10},{10... | collective-permute-start | bytes 1572872 | tf_op jit(solution)/shard_map/ppermute | solution.py:22
  66.1 0.3 all-to-all-done.blocks
  66.3 0.7 spread.2
  67.1 9.5 %all-to-all-start.1 = ((bf16[12,16,640]{2,1,0:T(8,128)(2,1)}), bf16[12,16,640]{2,1,0:T(8,128)(2,1)}, u32[]{:S(2)}, u32[]{:S(2)}) async-start(bf16[12,16,640]{2,1,0:T(8,128)(2,1)} %spread.2), calls=%async_computation.1 | async-start | bytes 491520 | tf_op jit(solution)/shard_map/all_to_all | solution.py:311
  76.6 0.0 copy-done.5
  76.6 0.0 copy-start.1
  76.6 0.4 own_part.1.part_own
  77.0 17.2 %all-to-all-done.1.blocks = bf16[12,16,640]{2,1,0:T(8,128)(2,1)} async-done(((bf16[12,16,640]{2,1,0:T(8,128)(2,1)}), bf16[12,16,640]{2,1,0:T(8,128)(2,1)}, u32[]{:S(2)}, u32[]{:S(2)}) %all-to-all-start.1) | async-done | bytes 245792 | tf_op jit(solution)/shard_map/all_to_all | solution.py:311
  94.3 1.6 %spread.3 = bf16[4,16,640]{2,1,0:T(8,128)(2,1)} custom-call(bf16[12,16,640]{2,1,0:T(8,128)(2,1)} %all-to-all-done.1.blocks), custom_call_target="tpu_custom_call" | custom-call | flops 1000000 | bytes 1000000 | tf_op jit(solution)/shard_map/spread/pallas_call | solution.py:196
  95.9 0.0 collective-permute-done.3.from_near
  95.9 0.0 collective-permute-done.4.from_far
  95.9 10.8 %all-to-all-start.2 = ((bf16[4,16,640]{2,1,0:T(8,128)(2,1)}), bf16[4,16,640]{2,1,0:T(8,128)(2,1)S(1)}, u32[]{:S(2)}, u32[]{:S(2)}) async-start(bf16[4,16,640]{2,1,0:T(8,128)(2,1)} %spread.3), calls=%async_computation.2 | async-start | bytes 163840 | tf_op jit(solution)/shard_map/all_to_all | solution.py:316
  106.7 0.0 copy-done.1
  106.7 2.8 %final.1 = bf16[512,512]{1,0:T(8,128)(2,1)} custom-call(f32[512,512]{1,0:T(8,128)S(1)} %own_part.1.part_own, bf16[512,512]{1,0:T(8,128)(2,1)} %collective-permute-done.3.from_near, bf16[512,512]{1,0:T(8,128)(2,1)} %collective-permute-done.4.from_far, f32[512,1]{1,0:T(8,128)S(1)} %copy.14.root, bf16[512,512]{1,0:T(8,128)(2,1)S(1)} %copy-done.1), custom_call_target="tpu_custom_call" | custom-call | flops 100000000 | bytes 1000000 | tf_op jit(solution)/shard_map/final/pallas_call | solution.py:272
  109.5 2.9 %all-to-all-done.2.refs_0_ = bf16[4,16,640]{2,1,0:T(8,128)(2,1)S(1)} async-done(((bf16[4,16,640]{2,1,0:T(8,128)(2,1)}), bf16[4,16,640]{2,1,0:T(8,128)(2,1)S(1)}, u32[]{:S(2)}, u32[]{:S(2)}) %all-to-all-start.2) | async-done | bytes 81952 | tf_op jit(solution)/shard_map/all_to_all | solution.py:316
  112.4 0.6 last_sum.1
  (1 shorter events, 0.0 us)
Async XLA Ops:
  0.6 21.2 %copy-start.6 = (s32[512]{0:T(512)S(1)}, s32[512]{0:T(512)}, u32[]{:S(2)}) copy-start(s32[512]{0:T(512)} %param.12) | copy-start | bytes 6148
  0.6 21.4 %copy-start.7 = (s32[4,6]{1,0:T(4,128)S(1)}, s32[4,6]{1,0:T(4,128)}, u32[]{:S(2)}) copy-start(s32[4,6]{1,0:T(4,128)} %param.10) | copy-start | bytes 292
  2.6 27.9 %collective-permute-start.1 = (bf16[512,512]{1,0:T(8,128)(2,1)S(1)}, bf16[512,512]{1,0:T(8,128)(2,1)S(1)}, u32[]{:S(2)}, u32[]{:S(2)}) collective-permute-start(bf16[512,512]{1,0:T(8,128)(2,1)S(1)} %multiply_convert_fusion.own), channel_id=1, source_target_pairs={{0,767},{1,2},{2,1},{3,4},{4,3},{5,6},{6,5},{7,8},{8,7},{9,10},{10... | collective-permute-start | bytes 1572872 | tf_op jit(solution)/shard_map/ppermute | solution.py:22
  18.7 20.0 %collective-permute-start = (bf16[512,512]{1,0:T(8,128)(2,1)S(1)}, bf16[512,512]{1,0:T(8,128)(2,1)S(1)}, u32[]{:S(2)}, u32[]{:S(2)}) collective-permute-start(bf16[512,512]{1,0:T(8,128)(2,1)S(1)} %multiply_convert_fusion.own), channel_id=1, source_target_pairs={{0,1},{1,0},{2,3},{3,2},{4,5},{5,4},{6,7},{7,6},{8,9},{9,8},{10,11... | collective-permute-start | bytes 1572872 | tf_op jit(solution)/shard_map/ppermute | solution.py:22
  22.0 16.7 %copy-start = (bf16[512,512]{1,0:T(8,128)(2,1)S(1)}, bf16[512,512]{1,0:T(8,128)(2,1)}, u32[]{:S(2)}) copy-start(bf16[512,512]{1,0:T(8,128)(2,1)} %weight.3) | copy-start | bytes 1572868
  22.0 16.7 %copy-start.2 = (bf16[512,512]{1,0:T(8,128)(2,1)S(1)}, bf16[512,512]{1,0:T(8,128)(2,1)}, u32[]{:S(2)}) copy-start(bf16[512,512]{1,0:T(8,128)(2,1)} %grad.1) | copy-start | bytes 1572868
  22.1 16.7 %copy-start.3 = (f32[512]{0:T(512)S(1)}, f32[512]{0:T(512)}, u32[]{:S(2)}) copy-start(f32[512]{0:T(512)} %param.9) | copy-start | bytes 6148
  28.6 13.7 %copy-start.4 = (bf16[512,512]{1,0:T(8,128)(2,1)}, bf16[512,512]{1,0:T(8,128)(2,1)S(1)}, u32[]{:S(2)}) copy-start(bf16[512,512]{1,0:T(8,128)(2,1)S(1)} %get-tuple-element.24.adj) | copy-start | bytes 1572868
  42.2 3.5 %collective-permute-start.2 = (bf16[256,640]{1,0:T(8,128)(2,1)S(1)}, bf16[256,640]{1,0:T(8,128)(2,1)S(1)}, u32[]{:S(2)}, u32[]{:S(2)}) collective-permute-start(bf16[256,640]{1,0:T(8,128)(2,1)S(1)} %get-tuple-element.23), channel_id=1, source_target_pairs={{0,24},{24,0},{1,25},{25,1},{2,26},{26,2},{3,27},{27,3},{4,28},{28... | collective-permute-start | bytes 983048 | tf_op jit(solution)/shard_map/ppermute | solution.py:22
  46.5 30.0 %copy-start.5 = (bf16[512,512]{1,0:T(8,128)(2,1)S(1)}, bf16[512,512]{1,0:T(8,128)(2,1)}, u32[]{:S(2)}) copy-start(bf16[512,512]{1,0:T(8,128)(2,1)} %copy-done.4) | copy-start | bytes 1572868
  46.5 19.8 %all-to-all-start = ((bf16[8,32,640]{2,1,0:T(8,128)(2,1)}), bf16[8,32,640]{2,1,0:T(8,128)(2,1)S(1)}, u32[]{:S(2)}, u32[]{:S(2)}) async-start(bf16[8,32,640]{2,1,0:T(8,128)(2,1)} %bitcast.4), calls=%async_computation | async-start | bytes 655360 | tf_op jit(solution)/shard_map/all_to_all | solution.py:310
  55.9 40.0 %collective-permute-start.3 = (bf16[512,512]{1,0:T(8,128)(2,1)}, bf16[512,512]{1,0:T(8,128)(2,1)}, u32[]{:S(2)}, u32[]{:S(2)}) collective-permute-start(bf16[512,512]{1,0:T(8,128)(2,1)} %get-tuple-element.29), channel_id=1, source_target_pairs={{0,1},{1,0},{2,3},{3,2},{4,5},{5,4},{6,7},{7,6},{8,9},{9,8},{10,11... | collective-permute-start | bytes 1572872 | tf_op jit(solution)/shard_map/ppermute | solution.py:22
  57.8 38.1 %collective-permute-start.4 = (bf16[512,512]{1,0:T(8,128)(2,1)}, bf16[512,512]{1,0:T(8,128)(2,1)}, u32[]{:S(2)}, u32[]{:S(2)}) collective-permute-start(bf16[512,512]{1,0:T(8,128)(2,1)} %get-tuple-element.30), channel_id=1, source_target_pairs={{0,767},{1,2},{2,1},{3,4},{4,3},{5,6},{6,5},{7,8},{8,7},{9,10},{10... | collective-permute-start | bytes 1572872 | tf_op jit(solution)/shard_map/ppermute | solution.py:22
  67.1 27.2 %all-to-all-start.1 = ((bf16[12,16,640]{2,1,0:T(8,128)(2,1)}), bf16[12,16,640]{2,1,0:T(8,128)(2,1)}, u32[]{:S(2)}, u32[]{:S(2)}) async-start(bf16[12,16,640]{2,1,0:T(8,128)(2,1)} %spread.2), calls=%async_computation.1 | async-start | bytes 491520 | tf_op jit(solution)/shard_map/all_to_all | solution.py:311
  76.6 30.1 %copy-start.1 = (bf16[512,512]{1,0:T(8,128)(2,1)S(1)}, bf16[512,512]{1,0:T(8,128)(2,1)}, u32[]{:S(2)}) copy-start(bf16[512,512]{1,0:T(8,128)(2,1)} %weight.3) | copy-start | bytes 1572868
  95.9 16.5 %all-to-all-start.2 = ((bf16[4,16,640]{2,1,0:T(8,128)(2,1)}), bf16[4,16,640]{2,1,0:T(8,128)(2,1)S(1)}, u32[]{:S(2)}, u32[]{:S(2)}) async-start(bf16[4,16,640]{2,1,0:T(8,128)(2,1)} %spread.3), calls=%async_computation.2 | async-start | bytes 163840 | tf_op jit(solution)/shard_map/all_to_all | solution.py:316

commit v4 on v3

--- a/solution.py
+++ b/solution.py
@@ -97,8 +97,8 @@
 
 
 def forward_kernel(
-    core_ref, adj, own, near, far, weight, bias, root, grad,
-    hidden, wsend, wkeep, scaled, agg_s, pre_s,
+    core_ref, adj, edge, own, near, far, weight, bias, root, grad,
+    hidden, wsend, wkeep, scaled, part_near, part_far, agg_s, pre_s,
 ):
     nodes, width = own.shape
     rows = 128
@@ -134,28 +134,6 @@
         def _():
             wsend[place, 0:width] = wgrad[band]
             wsend[place, width : width + 128] = bgrad[band]
-
-
-def forward(core, adj, own, near, far, weight, bias, root, grad):
-    nodes, width = own.shape
-    half = jax.ShapeDtypeStruct((width // 2, width + 128), bf16)
-    square = jax.ShapeDtypeStruct((nodes, width), bf16)
-    vmem = pl.BlockSpec(memory_space=pltpu.VMEM)
-    return pl.pallas_call(
-        forward_kernel,
-        in_specs=[pl.BlockSpec(memory_space=pltpu.SMEM)] + [vmem] * 8,
-        out_specs=[vmem] * 4,
-        out_shape=[square, half, half, square],
-        scratch_shapes=[pltpu.VMEM((nodes, width), bf16)] * 2,
-        compiler_params=pltpu.CompilerParams(vmem_limit_bytes=VMEM_LIMIT),
-        cost_estimate=pl.CostEstimate(flops=10**9, bytes_accessed=10**7, transcendentals=0),
-        name="forward",
-    )(core, adj, own, near, far, weight, bias, root, grad)
-
-
-def parts_kernel(edge, scaled, part_near, part_far):
-    nodes = scaled.shape[0]
-    rows = 128
     for first in range(0, nodes, rows):
         part = rows_dot(edge[first : first + rows, :], scaled[...])
         part_near[first : first + rows, :] = part.astype(bf16)
@@ -163,18 +141,21 @@
         part_far[first : first + rows, :] = part.astype(bf16)
 
 
-def parts(edge, scaled):
-    square = jax.ShapeDtypeStruct(scaled.shape, bf16)
-    vmem = pl.BlockSpec(memory_space=pltpu.VMEM)
-    return pl.pallas_call(
-        parts_kernel,
-        in_specs=[vmem] * 2,
-        out_specs=[vmem] * 2,
-        out_shape=[square, square],
-        compiler_params=pltpu.CompilerParams(vmem_limit_bytes=VMEM_LIMIT),
-        cost_estimate=pl.CostEstimate(flops=10**8, bytes_accessed=10**6, transcendentals=0),
-        name="parts",
-    )(edge, scaled)
+def forward(core, adj, edge, own, near, far, weight, bias, root, grad):
+    nodes, width = own.shape
+    half = jax.ShapeDtypeStruct((width // 2, width + 128), bf16)
+    square = jax.ShapeDtypeStruct((nodes, width), bf16)
+    vmem = pl.BlockSpec(memory_space=pltpu.VMEM)
+    return pl.pallas_call(
+        forward_kernel,
+        in_specs=[pl.BlockSpec(memory_space=pltpu.SMEM)] + [vmem] * 9,
+        out_specs=[vmem] * 6,
+        out_shape=[square, half, half, square, square, square],
+        scratch_shapes=[pltpu.VMEM((nodes, width), bf16)] * 2,
+        compiler_params=pltpu.CompilerParams(vmem_limit_bytes=VMEM_LIMIT),
+        cost_estimate=pl.CostEstimate(flops=10**9, bytes_accessed=10**7, transcendentals=0),
+        name="forward",
+    )(core, adj, edge, own, near, far, weight, bias, root, grad)
 
 
 def spread_kernel(blocks, out):
@@ -202,6 +183,56 @@
         cost_estimate=pl.CostEstimate(flops=10**6, bytes_accessed=10**6, transcendentals=0),
         name="spread",
     )(blocks)
+
+
+def halves_kernel(high_ref, blocks, sent, kept):
+    count = blocks.shape[0]
+    rows = sent.shape[0]
+    for half, out_type in ((1 - high_ref[0], "sent"), (high_ref[0], "kept")):
+        r = pl.ds(pl.multiple_of(half * rows, rows), rows)
+        total = blocks[0, r, :].astype(f32)
+        for i in range(1, count):
+            total += blocks[i, r, :].astype(f32)
+        if out_type == "sent":
+            sent[...] = total.astype(bf16)
+        else:
+            kept[...] = total
+
+
+def halves(high, blocks):
+    _, rows, width = blocks.shape
+    vmem = pl.BlockSpec(memory_space=pltpu.VMEM)
+    return pl.pallas_call(
+        halves_kernel,
+        in_specs=[pl.BlockSpec(memory_space=pltpu.SMEM), vmem],
+        out_specs=[vmem] * 2,
+        out_shape=[
+            jax.ShapeDtypeStruct((rows // 2, width), bf16),
+            jax.ShapeDtypeStruct((rows // 2, width), f32),
+        ],
+        compiler_params=pltpu.CompilerParams(vmem_limit_bytes=VMEM_LIMIT),
+        cost_estimate=pl.CostEstimate(flops=10**6, bytes_accessed=10**6, transcendentals=0),
+        name="halves",
+    )(high, blocks)
+
+
+def merge_kernel(kept, pair, out):
+    total = (kept[...] + pair[...].astype(f32)).astype(bf16)
+    for i in range(out.shape[0]):
+        out[i] = total
+
+
+def merge(kept, pair, copies):
+    vmem = pl.BlockSpec(memory_space=pltpu.VMEM)
+    return pl.pallas_call(
+        merge_kernel,
+        in_specs=[vmem] * 2,
+        out_specs=vmem,
+        out_shape=jax.ShapeDtypeStruct((copies, *kept.shape), bf16),
+        compiler_params=pltpu.CompilerParams(vmem_limit_bytes=VMEM_LIMIT),
+        cost_estimate=pl.CostEstimate(flops=10**6, bytes_accessed=10**6, transcendentals=0),
+        name="merge",
+    )(kept, pair)
 
 
 def last_sum_kernel(scale, blocks, out, bias):
@@ -298,22 +329,26 @@
     near = permute(own, NODE, near_partner)
     adj, edge, own_t = build_adjacency(local_slot, neighbours, counts)
     core = lax.axis_index("core").astype(jnp.int32).reshape(1)
-    hidden, wsend, wkeep, scaled = forward(
-        core, adj, own, near, far, weight, layer_bias[None, :], root, out_grad
+    hidden, wsend, wkeep, scaled, part_near, part_far = forward(
+        core, adj, edge, own, near, far, weight, layer_bias[None, :], root, out_grad
     )
     got = permute(wsend, "core", lambda i: i ^ 1)
-    part_near, part_far = parts(edge, scaled)
+    from_near = permute(part_near, NODE, near_partner)
+    ny, nx, nzl = (lax.axis_size(n) for n in ("y", "x", "zl"))
+    chip = (wkeep.astype(f32) + got.astype(f32)).astype(bf16)
+    part_far, chip = lax.optimization_barrier((part_far, chip))
     from_far = permute(part_far, NODE, far_partner)
-    from_near = permute(part_near, NODE, near_partner)
-    ny, nx, nzh, nzl = (lax.axis_size(n) for n in ("y", "x", "zh", "zl"))
-    chip = (wkeep.astype(f32) + got.astype(f32)).astype(bf16)
     blocks = lax.all_to_all(chip.reshape(ny, -1, width + 128), "y", 0, 0)
-    blocks = lax.all_to_all(spread(blocks, nzh, nzl), ("zh", "zl"), 0, 0)
+    own_t, from_near = lax.optimization_barrier((own_t, from_near))
     part_own = own_part(own_t, scaled)
     blocks, part_own = lax.optimization_barrier((blocks, part_own))
-    blocks = spread(blocks, 1, nx)
-    blocks, from_near, from_far = lax.optimization_barrier((blocks, from_near, from_far))
-    blocks = lax.all_to_all(blocks, "x", 0, 0)
+    blocks = lax.all_to_all(spread(blocks, 1, nx), "x", 0, 0)
+    high = lax.axis_index("zh").astype(jnp.int32).reshape(1)
+    sent, kept = halves(high, blocks)
+    pair = permute(sent, ("zh", "zl"), lambda i: -1 - i)
+    blocks = merge(kept, pair, nzl)
+    blocks, from_far = lax.optimization_barrier((blocks, from_far))
+    blocks = lax.all_to_all(blocks, "zl", 0, 0)
     weight_grad, bias_grad = last_sum(blocks, normaliser)
     input_grad = final(part_own, from_near, from_far, root, weight)
     return (hidden, input_grad, weight_grad, bias_grad[0])

time: 114 us -> 107 us (0.939)
  blocking collectives: 0 us -> 13.6 us
  waiting for transfers between devices: 32.1 us -> 21.5 us
  starting transfers between devices: 58.1 us -> 49.1 us
  Pallas kernels: 17.8 us -> 16.3 us
    all_to_all x2 -> x1, starting transfers between devices: 20.3 us -> 5.75 us  [local(): blocks = lax.all_to_all(blocks, 'zl', 0, 0)]
    all_to_all x0 -> x1, blocking collectives: none -> 13.6 us  [local(): blocks = lax.all_to_all(spread(blocks, 1, nx), 'x', 0, 0)]
    all_to_all x2 -> x1, waiting for transfers between devices: 20.1 us -> 6.71 us  [local(): blocks = lax.all_to_all(blocks, 'zl', 0, 0)]
    ppermute x5 -> x6, starting transfers between devices: 30.1 us -> 35.8 us  [permute(): lax.ppermute(array, axes, [(i, route(i) % peers) for i in range(peers)])]
    all_to_all x1, waiting for transfers between devices: 0.27 us -> 2.69 us  [local(): blocks = lax.all_to_all(chip.reshape(ny, -1, width + 128), 'y', 0, 0)]
    pallas_call x2 -> x1, Pallas kernels: 2.35 us -> 1.02 us  [spread(): pl.pallas_call(spread_kernel, in_specs=[vmem], out_specs=vmem, out_shape=...]
    ppermute x5 -> x6, waiting for transfers between devices: 11.8 us -> 12.1 us  [permute(): lax.ppermute(array, axes, [(i, route(i) % peers) for i in range(peers)])]
  transfers between devices with their start and end apart: 8 -> 8, of which waited for: 6 -> 5; matrix products, arithmetic and copies ran while one was open for 1% -> 2% of each run, Pallas kernels for 12% -> 11%
where the time goes in v4:
time: 107 us; the launch traced here: 106 us
  starting transfers between devices  49.1 us (46%)
  waiting for transfers between devices  21.5 us (20%)
  Pallas kernels  16.3 us (15%)
  blocking collectives  13.6 us (13%)
  other arithmetic  2.79 us (3%)
  local copies, waits for them, and re-layouts  2.09 us (2%)
    ppermute x6, starting transfers between devices, permute(): lax.ppermute(array, axes, [(i, route(i) % peers) for i in range(peers)])  35.8 us
    all_to_all x1, blocking collectives, local(): blocks = lax.all_to_all(spread(blocks, 1, nx), 'x', 0, 0)  13.6 us
    ppermute x6, waiting for transfers between devices, permute(): lax.ppermute(array, axes, [(i, route(i) % peers) for i in range(peers)])  12.1 us
    all_to_all x1, starting transfers between devices, local(): blocks = lax.all_to_all(chip.reshape(ny, -1, width + 128), 'y', 0, 0)  7.54 us
    all_to_all x1, waiting for transfers between devices, local(): blocks = lax.all_to_all(blocks, 'zl', 0, 0)  6.71 us
    pallas_call x1, Pallas kernels, build_adjacency(): pl.pallas_call(adjacency_kernel, grid=(tiles,), in_specs=[pl.BlockSpec(me...  6.48 us
    all_to_all x1, starting transfers between devices, local(): blocks = lax.all_to_all(blocks, 'zl', 0, 0)  5.75 us
    pallas_call x1, Pallas kernels, forward(): pl.pallas_call(forward_kernel, in_specs=[pl.BlockSpec(memory_space=pltpu....  4.33 us
  transfers between devices with their start and end apart: 8, of which 5 were waited for; matrix products, arithmetic and copies ran while one was open for 2% of the time, Pallas kernels for 11%

profile of v4, /device:TPU:8, one launch (start us, length us, event | category | flops | bytes accessed | tf_op | source)
XLA Modules:
  0.0 106.2 jit_solution(12945514574800205964)
XLA Ops:
  0.6 0.0 copy-start.6
  0.6 0.0 copy-start.7
  0.7 0.7 add_rsqrt_fusion
  1.4 1.2 %multiply_convert_fusion.own = bf16[512,512]{1,0:T(8,128)(2,1)S(1)} fusion(bf16[512,512]{1,0:T(8,128)(2,1)} %param.7, f32[512]{0:T(512)S(1)} %add_rsqrt_fusion), kind=kLoop, calls=%fused_computation | loop fusion | flops 786432 | bytes 1050624 | tf_op jit(solution)/shard_map/convert_element_type | solution.py:327
  2.6 16.1 %collective-permute-start.1 = (bf16[512,512]{1,0:T(8,128)(2,1)S(1)}, bf16[512,512]{1,0:T(8,128)(2,1)S(1)}, u32[]{:S(2)}, u32[]{:S(2)}) collective-permute-start(bf16[512,512]{1,0:T(8,128)(2,1)S(1)} %multiply_convert_fusion.own), channel_id=1, source_target_pairs={{0,767},{1,2},{2,1},{3,4},{4,3},{5,6},{6,5},{7,8},{8,7},{9,10},{10... | collective-permute-start | bytes 1572872 | tf_op jit(solution)/shard_map/ppermute | solution.py:22
  18.7 1.9 %collective-permute-start = (bf16[512,512]{1,0:T(8,128)(2,1)S(1)}, bf16[512,512]{1,0:T(8,128)(2,1)S(1)}, u32[]{:S(2)}, u32[]{:S(2)}) collective-permute-start(bf16[512,512]{1,0:T(8,128)(2,1)S(1)} %multiply_convert_fusion.own), channel_id=1, source_target_pairs={{0,1},{1,0},{2,3},{3,2},{4,5},{5,4},{6,7},{7,6},{8,9},{9,8},{10,11... | collective-permute-start | bytes 1572872 | tf_op jit(solution)/shard_map/ppermute | solution.py:22
  20.7 0.1 copy.14.root
  20.8 1.0 copy.12.nbr_ref
  21.8 0.0 copy-done.6
  21.8 0.1 copy.13.cnt_ref
  22.0 0.0 copy-done.7
  22.0 0.0 copy-start
  22.0 0.0 copy-start.4
  22.1 0.0 copy-start.5
  22.1 6.5 %adjacency.1 = (bf16[512,1536]{1,0:T(8,128)(2,1)S(1)}, bf16[1024,512]{1,0:T(8,128)(2,1)S(1)}, bf16[512,512]{1,0:T(8,128)(2,1)S(1)}) custom-call(s32[4,6]{1,0:T(4,128)S(1)} %add_select_fusion.slot_ref, s32[512,30]{1,0:T(8,128)S(1)} %copy.12.nbr_ref, s32[512,1]{1,0:T(8,128)S(1)} %copy.13.cnt_ref), custom_call_target="tpu_custom_call" | custom-call | flops 1000000000 | bytes 8000000 | tf_op jit(solution)/shard_map/adjacency/pallas_call | solution.py:75
  28.6 1.9 %collective-permute-done.1.far = bf16[512,512]{1,0:T(8,128)(2,1)S(1)} collective-permute-done((bf16[512,512]{1,0:T(8,128)(2,1)S(1)}, bf16[512,512]{1,0:T(8,128)(2,1)S(1)}, u32[]{:S(2)}, u32[]{:S(2)}) %collective-permute-start.1) | collective-permute-done | bytes 524320 | tf_op jit(solution)/shard_map/ppermute | solution.py:22
  30.5 8.3 %collective-permute-done.near = bf16[512,512]{1,0:T(8,128)(2,1)S(1)} collective-permute-done((bf16[512,512]{1,0:T(8,128)(2,1)S(1)}, bf16[512,512]{1,0:T(8,128)(2,1)S(1)}, u32[]{:S(2)}, u32[]{:S(2)}) %collective-permute-start) | collective-permute-done | bytes 524320 | tf_op jit(solution)/shard_map/ppermute | solution.py:22
  38.7 0.0 copy-done
  38.7 0.0 copy-done.4
  38.7 0.0 copy-done.5
  38.7 4.3 %forward.1 = (bf16[512,512]{1,0:T(8,128)(2,1)}, bf16[256,640]{1,0:T(8,128)(2,1)S(1)}, bf16[256,640]{1,0:T(8,128)(2,1)S(1)}, bf16[512,512]{1,0:T(8,128)(2,1)S(1)}...) custom-call(s32[1]{0:T(128)} %bitcast.core_ref, bf16[512,1536]{1,0:T(8,128)(2,1)S(1)} %get-tuple-element.25.adj, ...), custom_call_target="tpu_custom_call" | custom-call | flops 1000000000 | bytes 10000000 | tf_op jit(solution)/shard_map/forward/pallas_call | solution.py:149
  43.1 1.9 %collective-permute-start.2 = (bf16[256,640]{1,0:T(8,128)(2,1)S(1)}, bf16[256,640]{1,0:T(8,128)(2,1)S(1)}, u32[]{:S(2)}, u32[]{:S(2)}) collective-permute-start(bf16[256,640]{1,0:T(8,128)(2,1)S(1)} %get-tuple-element.30), channel_id=1, source_target_pairs={{0,24},{24,0},{1,25},{25,1},{2,26},{26,2},{3,27},{27,3},{4,28},{28... | collective-permute-start | bytes 983048 | tf_op jit(solution)/shard_map/ppermute | solution.py:22
  45.0 1.9 %collective-permute-start.3 = (bf16[512,512]{1,0:T(8,128)(2,1)S(1)}, bf16[512,512]{1,0:T(8,128)(2,1)S(1)}, u32[]{:S(2)}, u32[]{:S(2)}) collective-permute-start(bf16[512,512]{1,0:T(8,128)(2,1)S(1)} %get-tuple-element.33), channel_id=1, source_target_pairs={{0,1},{1,0},{2,3},{3,2},{4,5},{5,4},{6,7},{7,6},{8,9},{9,8},{10,11... | collective-permute-start | bytes 1572872 | tf_op jit(solution)/shard_map/ppermute | solution.py:22
  46.9 0.0 collective-permute-done.2
  46.9 0.8 add_convert_fusion
  47.8 7.5 %all-to-all-start = ((bf16[8,32,640]{2,1,0:T(8,128)(2,1)}), bf16[8,32,640]{2,1,0:T(8,128)(2,1)}, u32[]{:S(2)}, u32[]{:S(2)}) async-start(bf16[8,32,640]{2,1,0:T(8,128)(2,1)} %bitcast.4), calls=%async_computation | async-start | bytes 655360 | tf_op jit(solution)/shard_map/all_to_all | solution.py:341
  55.3 8.6 %collective-permute-start.5 = (bf16[512,512]{1,0:T(8,128)(2,1)}, bf16[512,512]{1,0:T(8,128)(2,1)}, u32[]{:S(2)}, u32[]{:S(2)}) collective-permute-start(bf16[512,512]{1,0:T(8,128)(2,1)} %get-tuple-element.41), channel_id=1, source_target_pairs={{0,767},{1,2},{2,1},{3,4},{4,3},{5,6},{6,5},{7,8},{8,7},{9,10},{10... | collective-permute-start | bytes 1572872 | tf_op jit(solution)/shard_map/ppermute | solution.py:22
  63.9 0.0 collective-permute-done.3.from_near
  63.9 0.0 copy-start.2
  63.9 0.8 copy-done.2
  64.7 0.4 own_part.1.part_own
  65.2 0.0 copy-start.1
  65.2 0.0 copy-start.3
  65.2 2.7 %all-to-all-done.blocks = bf16[8,32,640]{2,1,0:T(8,128)(2,1)} async-done(((bf16[8,32,640]{2,1,0:T(8,128)(2,1)}), bf16[8,32,640]{2,1,0:T(8,128)(2,1)}, u32[]{:S(2)}, u32[]{:S(2)}) %all-to-all-start) | async-done | bytes 327712 | tf_op jit(solution)/shard_map/all_to_all | solution.py:341
  67.9 1.0 spread.1
  68.9 13.6 %all_to_all.15.blocks = bf16[4,32,640]{2,1,0:T(8,128)(2,1)S(1)} all-to-all(bf16[4,32,640]{2,1,0:T(8,128)(2,1)S(1)} %spread.1), channel_id=1, replica_groups=mesh['y'=8,'zh'=2,'core'=2,'x'=4,'zl'=6] {'x'}, dimensions={0} | all-to-all | bytes 327680 | tf_op jit(solution)/shard_map/all_to_all | solution.py:345
  82.5 5.3 %collective-permute-start.4 = (bf16[16,640]{1,0:T(8,128)(2,1)S(1)}, bf16[16,640]{1,0:T(8,128)(2,1)S(1)}, u32[]{:S(2)}, u32[]{:S(2)}) collective-permute-start(bf16[16,640]{1,0:T(8,128)(2,1)S(1)} %get-tuple-element.40), channel_id=1, source_target_pairs={{0,53},{1,52},{2,51},{3,50},{4,49},{5,48},{48,5},{49,4},{50,3},{51... | collective-permute-start | bytes 61448 | tf_op jit(solution)/shard_map/ppermute | solution.py:22
  87.8 1.9 %collective-permute-done.4.pair = bf16[16,640]{1,0:T(8,128)(2,1)S(1)} collective-permute-done((bf16[16,640]{1,0:T(8,128)(2,1)S(1)}, bf16[16,640]{1,0:T(8,128)(2,1)S(1)}, u32[]{:S(2)}, u32[]{:S(2)}) %collective-permute-start.4) | collective-permute-done | bytes 20512 | tf_op jit(solution)/shard_map/ppermute | solution.py:22
  89.8 0.7 merge.1
  90.4 0.0 collective-permute-done.5.from_far
  90.4 5.7 %all-to-all-start.2 = ((bf16[6,16,640]{2,1,0:T(8,128)(2,1)}), bf16[6,16,640]{2,1,0:T(8,128)(2,1)S(1)}, u32[]{:S(2)}, u32[]{:S(2)}) async-start(bf16[6,16,640]{2,1,0:T(8,128)(2,1)} %merge.1), calls=%async_computation.2 | async-start | bytes 245760 | tf_op jit(solution)/shard_map/all_to_all | solution.py:351
  96.2 0.0 copy-done.1
  96.2 0.0 copy-done.3
  96.2 2.7 %final.1 = bf16[512,512]{1,0:T(8,128)(2,1)} custom-call(f32[512,512]{1,0:T(8,128)S(1)} %own_part.1.part_own, bf16[512,512]{1,0:T(8,128)(2,1)S(1)} %copy-done.3, bf16[512,512]{1,0:T(8,128)(2,1)} %collective-permute-done.5.from_far, f32[512,1]{1,0:T(8,128)S(1)} %copy.14.root, bf16[512,512]{1,0:T(8,128)(2,1)S(1)} %copy-done.1), custom_call_target="tpu_custom_call" | custom-call | flops 100000000 | bytes 1000000 | tf_op jit(solution)/shard_map/final/pallas_call | solution.py:303
  98.9 6.7 %all-to-all-done.2.refs_0_ = bf16[6,16,640]{2,1,0:T(8,128)(2,1)S(1)} async-done(((bf16[6,16,640]{2,1,0:T(8,128)(2,1)}), bf16[6,16,640]{2,1,0:T(8,128)(2,1)S(1)}, u32[]{:S(2)}, u32[]{:S(2)}) %all-to-all-start.2) | async-done | bytes 122912 | tf_op jit(solution)/shard_map/all_to_all | solution.py:351
  105.6 0.6 last_sum.1
  (2 shorter events, 0.0 us)
Async XLA Ops:
  0.6 21.2 %copy-start.6 = (s32[512]{0:T(512)S(1)}, s32[512]{0:T(512)}, u32[]{:S(2)}) copy-start(s32[512]{0:T(512)} %param.12) | copy-start | bytes 6148
  0.6 21.4 %copy-start.7 = (s32[4,6]{1,0:T(4,128)S(1)}, s32[4,6]{1,0:T(4,128)}, u32[]{:S(2)}) copy-start(s32[4,6]{1,0:T(4,128)} %param.10) | copy-start | bytes 292
  2.6 27.9 %collective-permute-start.1 = (bf16[512,512]{1,0:T(8,128)(2,1)S(1)}, bf16[512,512]{1,0:T(8,128)(2,1)S(1)}, u32[]{:S(2)}, u32[]{:S(2)}) collective-permute-start(bf16[512,512]{1,0:T(8,128)(2,1)S(1)} %multiply_convert_fusion.own), channel_id=1, source_target_pairs={{0,767},{1,2},{2,1},{3,4},{4,3},{5,6},{6,5},{7,8},{8,7},{9,10},{10... | collective-permute-start | bytes 1572872 | tf_op jit(solution)/shard_map/ppermute | solution.py:22
  18.7 20.0 %collective-permute-start = (bf16[512,512]{1,0:T(8,128)(2,1)S(1)}, bf16[512,512]{1,0:T(8,128)(2,1)S(1)}, u32[]{:S(2)}, u32[]{:S(2)}) collective-permute-start(bf16[512,512]{1,0:T(8,128)(2,1)S(1)} %multiply_convert_fusion.own), channel_id=1, source_target_pairs={{0,1},{1,0},{2,3},{3,2},{4,5},{5,4},{6,7},{7,6},{8,9},{9,8},{10,11... | collective-permute-start | bytes 1572872 | tf_op jit(solution)/shard_map/ppermute | solution.py:22
  22.0 16.7 %copy-start = (bf16[512,512]{1,0:T(8,128)(2,1)S(1)}, bf16[512,512]{1,0:T(8,128)(2,1)}, u32[]{:S(2)}) copy-start(bf16[512,512]{1,0:T(8,128)(2,1)} %weight.3) | copy-start | bytes 1572868
  22.0 16.7 %copy-start.4 = (bf16[512,512]{1,0:T(8,128)(2,1)S(1)}, bf16[512,512]{1,0:T(8,128)(2,1)}, u32[]{:S(2)}) copy-start(bf16[512,512]{1,0:T(8,128)(2,1)} %grad.1) | copy-start | bytes 1572868
  22.1 16.7 %copy-start.5 = (f32[512]{0:T(512)S(1)}, f32[512]{0:T(512)}, u32[]{:S(2)}) copy-start(f32[512]{0:T(512)} %param.9) | copy-start | bytes 6148
  43.1 3.9 %collective-permute-start.2 = (bf16[256,640]{1,0:T(8,128)(2,1)S(1)}, bf16[256,640]{1,0:T(8,128)(2,1)S(1)}, u32[]{:S(2)}, u32[]{:S(2)}) collective-permute-start(bf16[256,640]{1,0:T(8,128)(2,1)S(1)} %get-tuple-element.30), channel_id=1, source_target_pairs={{0,24},{24,0},{1,25},{25,1},{2,26},{26,2},{3,27},{27,3},{4,28},{28... | collective-permute-start | bytes 983048 | tf_op jit(solution)/shard_map/ppermute | solution.py:22
  45.0 18.9 %collective-permute-start.3 = (bf16[512,512]{1,0:T(8,128)(2,1)S(1)}, bf16[512,512]{1,0:T(8,128)(2,1)S(1)}, u32[]{:S(2)}, u32[]{:S(2)}) collective-permute-start(bf16[512,512]{1,0:T(8,128)(2,1)S(1)} %get-tuple-element.33), channel_id=1, source_target_pairs={{0,1},{1,0},{2,3},{3,2},{4,5},{5,4},{6,7},{7,6},{8,9},{9,8},{10,11... | collective-permute-start | bytes 1572872 | tf_op jit(solution)/shard_map/ppermute | solution.py:22
  47.8 20.1 %all-to-all-start = ((bf16[8,32,640]{2,1,0:T(8,128)(2,1)}), bf16[8,32,640]{2,1,0:T(8,128)(2,1)}, u32[]{:S(2)}, u32[]{:S(2)}) async-start(bf16[8,32,640]{2,1,0:T(8,128)(2,1)} %bitcast.4), calls=%async_computation | async-start | bytes 655360 | tf_op jit(solution)/shard_map/all_to_all | solution.py:341
  55.3 35.1 %collective-permute-start.5 = (bf16[512,512]{1,0:T(8,128)(2,1)}, bf16[512,512]{1,0:T(8,128)(2,1)}, u32[]{:S(2)}, u32[]{:S(2)}) collective-permute-start(bf16[512,512]{1,0:T(8,128)(2,1)} %get-tuple-element.41), channel_id=1, source_target_pairs={{0,767},{1,2},{2,1},{3,4},{4,3},{5,6},{6,5},{7,8},{8,7},{9,10},{10... | collective-permute-start | bytes 1572872 | tf_op jit(solution)/shard_map/ppermute | solution.py:22
  63.9 0.8 copy-start.2
  65.2 31.0 %copy-start.1 = (bf16[512,512]{1,0:T(8,128)(2,1)S(1)}, bf16[512,512]{1,0:T(8,128)(2,1)}, u32[]{:S(2)}) copy-start(bf16[512,512]{1,0:T(8,128)(2,1)} %weight.3) | copy-start | bytes 1572868
  65.2 31.0 %copy-start.3 = (bf16[512,512]{1,0:T(8,128)(2,1)S(1)}, bf16[512,512]{1,0:T(8,128)(2,1)}, u32[]{:S(2)}) copy-start(bf16[512,512]{1,0:T(8,128)(2,1)} %copy-done.2) | copy-start | bytes 1572868
  82.5 7.3 %collective-permute-start.4 = (bf16[16,640]{1,0:T(8,128)(2,1)S(1)}, bf16[16,640]{1,0:T(8,128)(2,1)S(1)}, u32[]{:S(2)}, u32[]{:S(2)}) collective-permute-start(bf16[16,640]{1,0:T(8,128)(2,1)S(1)} %get-tuple-element.40), channel_id=1, source_target_pairs={{0,53},{1,52},{2,51},{3,50},{4,49},{5,48},{48,5},{49,4},{50,3},{51... | collective-permute-start | bytes 61448 | tf_op jit(solution)/shard_map/ppermute | solution.py:22
  90.4 15.1 %all-to-all-start.2 = ((bf16[6,16,640]{2,1,0:T(8,128)(2,1)}), bf16[6,16,640]{2,1,0:T(8,128)(2,1)S(1)}, u32[]{:S(2)}, u32[]{:S(2)}) async-start(bf16[6,16,640]{2,1,0:T(8,128)(2,1)} %merge.1), calls=%async_computation.2 | async-start | bytes 245760 | tf_op jit(solution)/shard_map/all_to_all | solution.py:351

commit v5 on v4

--- a/solution.py
+++ b/solution.py
@@ -97,8 +97,8 @@
 
 
 def forward_kernel(
-    core_ref, adj, edge, own, near, far, weight, bias, root, grad,
-    hidden, wsend, wkeep, scaled, part_near, part_far, agg_s, pre_s,
+    core_ref, adj, own, near, far, weight, bias, root, grad,
+    hidden, wsend, wkeep, scaled, agg_s, pre_s,
 ):
     nodes, width = own.shape
     rows = 128
@@ -134,6 +134,28 @@
         def _():
             wsend[place, 0:width] = wgrad[band]
             wsend[place, width : width + 128] = bgrad[band]
+
+
+def forward(core, adj, own, near, far, weight, bias, root, grad):
+    nodes, width = own.shape
+    half = jax.ShapeDtypeStruct((width // 2, width + 128), bf16)
+    square = jax.ShapeDtypeStruct((nodes, width), bf16)
+    vmem = pl.BlockSpec(memory_space=pltpu.VMEM)
+    return pl.pallas_call(
+        forward_kernel,
+        in_specs=[pl.BlockSpec(memory_space=pltpu.SMEM)] + [vmem] * 8,
+        out_specs=[vmem] * 4,
+        out_shape=[square, half, half, square],
+        scratch_shapes=[pltpu.VMEM((nodes, width), bf16)] * 2,
+        compiler_params=pltpu.CompilerParams(vmem_limit_bytes=VMEM_LIMIT),
+        cost_estimate=pl.CostEstimate(flops=10**9, bytes_accessed=10**7, transcendentals=0),
+        name="forward",
+    )(core, adj, own, near, far, weight, bias, root, grad)
+
+
+def parts_kernel(edge, scaled, part_near, part_far):
+    nodes = scaled.shape[0]
+    rows = 128
     for first in range(0, nodes, rows):
         part = rows_dot(edge[first : first + rows, :], scaled[...])
         part_near[first : first + rows, :] = part.astype(bf16)
@@ -141,21 +163,18 @@
         part_far[first : first + rows, :] = part.astype(bf16)
 
 
-def forward(core, adj, edge, own, near, far, weight, bias, root, grad):
-    nodes, width = own.shape
-    half = jax.ShapeDtypeStruct((width // 2, width + 128), bf16)
-    square = jax.ShapeDtypeStruct((nodes, width), bf16)
-    vmem = pl.BlockSpec(memory_space=pltpu.VMEM)
-    return pl.pallas_call(
-        forward_kernel,
-        in_specs=[pl.BlockSpec(memory_space=pltpu.SMEM)] + [vmem] * 9,
-        out_specs=[vmem] * 6,
-        out_shape=[square, half, half, square, square, square],
-        scratch_shapes=[pltpu.VMEM((nodes, width), bf16)] * 2,
-        compiler_params=pltpu.CompilerParams(vmem_limit_bytes=VMEM_LIMIT),
-        cost_estimate=pl.CostEstimate(flops=10**9, bytes_accessed=10**7, transcendentals=0),
-        name="forward",
-    )(core, adj, edge, own, near, far, weight, bias, root, grad)
+def parts(edge, scaled):
+    square = jax.ShapeDtypeStruct(scaled.shape, bf16)
+    vmem = pl.BlockSpec(memory_space=pltpu.VMEM)
+    return pl.pallas_call(
+        parts_kernel,
+        in_specs=[vmem] * 2,
+        out_specs=[vmem] * 2,
+        out_shape=[square, square],
+        compiler_params=pltpu.CompilerParams(vmem_limit_bytes=VMEM_LIMIT),
+        cost_estimate=pl.CostEstimate(flops=10**8, bytes_accessed=10**6, transcendentals=0),
+        name="parts",
+    )(edge, scaled)
 
 
 def spread_kernel(blocks, out):
@@ -281,7 +300,7 @@
         out_specs=vmem,
         out_shape=jax.ShapeDtypeStruct(scaled.shape, f32),
         compiler_params=pltpu.CompilerParams(vmem_limit_bytes=VMEM_LIMIT),
-        cost_estimate=pl.CostEstimate(flops=10**12, bytes_accessed=10**9, transcendentals=0),
+        cost_estimate=pl.CostEstimate(flops=10**8, bytes_accessed=10**6, transcendentals=0),
         name="own_part",
     )(adj, scaled)
 
@@ -329,25 +348,24 @@
     near = permute(own, NODE, near_partner)
     adj, edge, own_t = build_adjacency(local_slot, neighbours, counts)
     core = lax.axis_index("core").astype(jnp.int32).reshape(1)
-    hidden, wsend, wkeep, scaled, part_near, part_far = forward(
-        core, adj, edge, own, near, far, weight, layer_bias[None, :], root, out_grad
+    hidden, wsend, wkeep, scaled = forward(
+        core, adj, own, near, far, weight, layer_bias[None, :], root, out_grad
     )
     got = permute(wsend, "core", lambda i: i ^ 1)
-    from_near = permute(part_near, NODE, near_partner)
     ny, nx, nzl = (lax.axis_size(n) for n in ("y", "x", "zl"))
     chip = (wkeep.astype(f32) + got.astype(f32)).astype(bf16)
-    part_far, chip = lax.optimization_barrier((part_far, chip))
+    scaled, chip = lax.optimization_barrier((scaled, chip))
+    part_near, part_far = parts(edge, scaled)
+    from_near = permute(part_near, NODE, near_partner)
     from_far = permute(part_far, NODE, far_partner)
     blocks = lax.all_to_all(chip.reshape(ny, -1, width + 128), "y", 0, 0)
-    own_t, from_near = lax.optimization_barrier((own_t, from_near))
     part_own = own_part(own_t, scaled)
-    blocks, part_own = lax.optimization_barrier((blocks, part_own))
     blocks = lax.all_to_all(spread(blocks, 1, nx), "x", 0, 0)
     high = lax.axis_index("zh").astype(jnp.int32).reshape(1)
     sent, kept = halves(high, blocks)
     pair = permute(sent, ("zh", "zl"), lambda i: -1 - i)
     blocks = merge(kept, pair, nzl)
-    blocks, from_far = lax.optimization_barrier((blocks, from_far))
+    blocks, from_near, from_far = lax.optimization_barrier((blocks, from_near, from_far))
     blocks = lax.all_to_all(blocks, "zl", 0, 0)
     weight_grad, bias_grad = last_sum(blocks, normaliser)
     input_grad = final(part_own, from_near, from_far, root, weight)

time: 107 us -> 114 us (1.065)
  the two profiles are of different devices: /device:TPU:8 before, /device:TPU:64 now
where the time goes in v5:
time: 114 us; the launch traced here: 113 us
  starting transfers between devices  59.5 us (52%)
  waiting for transfers between devices  15.8 us (14%)
  Pallas kernels  15 us (13%)
  blocking collectives  12.2 us (11%)
  local copies, waits for them, and re-layouts  7.24 us (6%)
  other arithmetic  2.79 us (2%)
    ppermute x6, starting transfers between devices, permute(): lax.ppermute(array, axes, [(i, route(i) % peers) for i in range(peers)])  36.5 us
    all_to_all x1, starting transfers between devices, local(): blocks = lax.all_to_all(blocks, 'zl', 0, 0)  16 us
    all_to_all x1, blocking collectives, local(): blocks = lax.all_to_all(spread(blocks, 1, nx), 'x', 0, 0)  12.2 us
    all_to_all x1, starting transfers between devices, local(): blocks = lax.all_to_all(chip.reshape(ny, -1, width + 128), 'y', 0, 0)  7.1 us
    pallas_call x1, Pallas kernels, build_adjacency(): pl.pallas_call(adjacency_kernel, grid=(tiles,), in_specs=[pl.BlockSpec(me...  6.46 us
    unnamed x23, local copies, waits for them, and re-layouts  6.23 us
    all_to_all x1, waiting for transfers between devices, local(): blocks = lax.all_to_all(blocks, 'zl', 0, 0)  6.14 us
    all_to_all x1, waiting for transfers between devices, local(): blocks = lax.all_to_all(chip.reshape(ny, -1, width + 128), 'y', 0, 0)  5.63 us
  transfers between devices with their start and end apart: 8, of which 5 were waited for; matrix products, arithmetic and copies ran while one was open for 2% of the time, Pallas kernels for 10%

profile of v5, /device:TPU:64, one launch (start us, length us, event | category | flops | bytes accessed | tf_op | source)
XLA Modules:
  0.0 113.3 jit_solution(153954827650194890)
XLA Ops:
  0.6 0.0 copy-start.9
  0.6 0.0 copy-start.10
  0.7 0.7 add_rsqrt_fusion
  1.4 1.2 %multiply_convert_fusion.own = bf16[512,512]{1,0:T(8,128)(2,1)S(1)} fusion(bf16[512,512]{1,0:T(8,128)(2,1)} %param.7, f32[512]{0:T(512)S(1)} %add_rsqrt_fusion), kind=kLoop, calls=%fused_computation | loop fusion | flops 786432 | bytes 1050624 | tf_op jit(solution)/shard_map/convert_element_type | solution.py:346
  2.6 4.3 %collective-permute-start.1 = (bf16[512,512]{1,0:T(8,128)(2,1)S(1)}, bf16[512,512]{1,0:T(8,128)(2,1)S(1)}, u32[]{:S(2)}, u32[]{:S(2)}) collective-permute-start(bf16[512,512]{1,0:T(8,128)(2,1)S(1)} %multiply_convert_fusion.own), channel_id=1, source_target_pairs={{0,767},{1,2},{2,1},{3,4},{4,3},{5,6},{6,5},{7,8},{8,7},{9,10},{10... | collective-permute-start | bytes 1572872 | tf_op jit(solution)/shard_map/ppermute | solution.py:22
  6.9 16.4 %collective-permute-start = (bf16[512,512]{1,0:T(8,128)(2,1)S(1)}, bf16[512,512]{1,0:T(8,128)(2,1)S(1)}, u32[]{:S(2)}, u32[]{:S(2)}) collective-permute-start(bf16[512,512]{1,0:T(8,128)(2,1)S(1)} %multiply_convert_fusion.own), channel_id=1, source_target_pairs={{0,1},{1,0},{2,3},{3,2},{4,5},{5,4},{6,7},{7,6},{8,9},{9,8},{10,11... | collective-permute-start | bytes 1572872 | tf_op jit(solution)/shard_map/ppermute | solution.py:22
  23.4 0.1 copy.14.root
  23.5 1.7 %copy.12.nbr_ref = s32[512,30]{1,0:T(8,128)} copy(s32[512,30]{0,1:T(8,128)} %param.11) | data formatting | bytes 122880 | tf_op args[4]
  25.2 0.0 copy-done.9
  25.2 0.9 copy.13.cnt_ref
  26.1 0.0 copy-done.10
  26.1 0.0 copy-start.6
  26.1 0.9 copy-done.6
  27.0 0.0 copy-start.7
  27.0 0.9 copy-done.7
  28.0 0.0 copy-start
  28.0 0.0 copy-start.1
  28.0 0.0 copy-start.8
  28.0 6.5 %adjacency.1 = (bf16[512,1536]{1,0:T(8,128)(2,1)S(1)}, bf16[1024,512]{1,0:T(8,128)(2,1)S(1)}, bf16[512,512]{1,0:T(8,128)(2,1)S(1)}) custom-call(s32[4,6]{1,0:T(4,128)S(1)} %add_select_fusion.slot_ref, s32[512,30]{1,0:T(8,128)S(1)} %copy-done.6, s32[512,1]{1,0:T(8,128)S(1)} %copy-done.7), custom_call_target="tpu_custom_call" | custom-call | flops 1000000000 | bytes 8000000 | tf_op jit(solution)/shard_map/adjacency/pallas_call | solution.py:75
  34.5 0.0 copy-start.4
  34.5 0.8 copy-done.4
  35.3 0.0 collective-permute-done.1.far
  35.3 0.6 collective-permute-done.near
  35.9 0.0 copy-start.2
  35.9 0.8 copy-done.2
  36.7 0.0 copy-done
  36.7 0.0 copy-done.1
  36.7 0.0 copy-done.8
  36.7 0.0 copy-start.3
  36.7 1.0 copy-done.3
  37.7 3.5 %forward.1 = (bf16[512,512]{1,0:T(8,128)(2,1)}, bf16[256,640]{1,0:T(8,128)(2,1)S(1)}, bf16[256,640]{1,0:T(8,128)(2,1)S(1)}, bf16[512,512]{1,0:T(8,128)(2,1)S(1)}) custom-call(s32[1]{0:T(128)} %bitcast.core_ref, bf16[512,1536]{1,0:T(8,128)(2,1)S(1)} %get-tuple-element.22.adj, bf16[512,512]{1,0:T(8,128)(2,1)S(1)} %multiply_convert_fusion.own, ...), custom_call_target="tpu_custom_call" | custom-call | flops 1000000000 | bytes 10000000 | tf_op jit(solution)/shard_map/forward/pallas_call | solution.py:144
  41.2 1.9 %collective-permute-start.2 = (bf16[256,640]{1,0:T(8,128)(2,1)S(1)}, bf16[256,640]{1,0:T(8,128)(2,1)S(1)}, u32[]{:S(2)}, u32[]{:S(2)}) collective-permute-start(bf16[256,640]{1,0:T(8,128)(2,1)S(1)} %get-tuple-element.27), channel_id=1, source_target_pairs={{0,24},{24,0},{1,25},{25,1},{2,26},{26,2},{3,27},{27,3},{4,28},{28... | collective-permute-start | bytes 983048 | tf_op jit(solution)/shard_map/ppermute | solution.py:22
  43.1 1.6 %collective-permute-done.2 = bf16[256,640]{1,0:T(8,128)(2,1)S(1)} collective-permute-done((bf16[256,640]{1,0:T(8,128)(2,1)S(1)}, bf16[256,640]{1,0:T(8,128)(2,1)S(1)}, u32[]{:S(2)}, u32[]{:S(2)}) %collective-permute-start.2) | collective-permute-done | bytes 327712 | tf_op jit(solution)/shard_map/ppermute | solution.py:22
  44.7 0.8 add_convert_fusion
  45.5 7.1 %all-to-all-start = ((bf16[8,32,640]{2,1,0:T(8,128)(2,1)}), bf16[8,32,640]{2,1,0:T(8,128)(2,1)S(1)}, u32[]{:S(2)}, u32[]{:S(2)}) async-start(bf16[8,32,640]{2,1,0:T(8,128)(2,1)} %bitcast.5), calls=%async_computation | async-start | bytes 655360 | tf_op jit(solution)/shard_map/all_to_all | solution.py:361
  52.6 0.0 copy-start.5
  52.6 1.6 %parts.1 = (bf16[512,512]{1,0:T(8,128)(2,1)}, bf16[512,512]{1,0:T(8,128)(2,1)}) custom-call(bf16[1024,512]{1,0:T(8,128)(2,1)S(1)} %get-tuple-element.32.edge, bf16[512,512]{1,0:T(8,128)(2,1)S(1)} %get-tuple-element.28.scaled), custom_call_target="tpu_custom_call" | custom-call | flops 100000000 | bytes 1000000 | tf_op jit(solution)/shard_map/parts/pallas_call | solution.py:169
  54.3 4.4 %collective-permute-start.4 = (bf16[512,512]{1,0:T(8,128)(2,1)}, bf16[512,512]{1,0:T(8,128)(2,1)S(1)}, u32[]{:S(2)}, u32[]{:S(2)}) collective-permute-start(bf16[512,512]{1,0:T(8,128)(2,1)} %get-tuple-element.33), channel_id=1, source_target_pairs={{0,1},{1,0},{2,3},{3,2},{4,5},{5,4},{6,7},{7,6},{8,9},{9,8},{10,11... | collective-permute-start | bytes 1572872 | tf_op jit(solution)/shard_map/ppermute | solution.py:22
  58.7 1.9 %collective-permute-start.5 = (bf16[512,512]{1,0:T(8,128)(2,1)}, bf16[512,512]{1,0:T(8,128)(2,1)S(1)}, u32[]{:S(2)}, u32[]{:S(2)}) collective-permute-start(bf16[512,512]{1,0:T(8,128)(2,1)} %get-tuple-element.34), channel_id=1, source_target_pairs={{0,767},{1,2},{2,1},{3,4},{4,3},{5,6},{6,5},{7,8},{8,7},{9,10},{10... | collective-permute-start | bytes 1572872 | tf_op jit(solution)/shard_map/ppermute | solution.py:22
  60.6 5.6 %all-to-all-done.blocks = bf16[8,32,640]{2,1,0:T(8,128)(2,1)S(1)} async-done(((bf16[8,32,640]{2,1,0:T(8,128)(2,1)}), bf16[8,32,640]{2,1,0:T(8,128)(2,1)S(1)}, u32[]{:S(2)}, u32[]{:S(2)}) %all-to-all-start) | async-done | bytes 327712 | tf_op jit(solution)/shard_map/all_to_all | solution.py:361
  66.3 12.2 %all_to_all.15.blocks = bf16[4,32,640]{2,1,0:T(8,128)(2,1)S(1)} all-to-all(bf16[4,32,640]{2,1,0:T(8,128)(2,1)S(1)} %spread.1), channel_id=1, replica_groups=mesh['y'=8,'zh'=2,'core'=2,'x'=4,'zl'=6] {'x'}, dimensions={0} | all-to-all | bytes 327680 | tf_op jit(solution)/shard_map/all_to_all | solution.py:363
  78.5 7.6 %collective-permute-start.3 = (bf16[16,640]{1,0:T(8,128)(2,1)S(1)}, bf16[16,640]{1,0:T(8,128)(2,1)S(1)}, u32[]{:S(2)}, u32[]{:S(2)}) collective-permute-start(bf16[16,640]{1,0:T(8,128)(2,1)S(1)} %get-tuple-element.31), channel_id=1, source_target_pairs={{0,53},{1,52},{2,51},{3,50},{4,49},{5,48},{48,5},{49,4},{50,3},{51... | collective-permute-start | bytes 61448 | tf_op jit(solution)/shard_map/ppermute | solution.py:22
  86.1 1.7 %collective-permute-done.3.pair = bf16[16,640]{1,0:T(8,128)(2,1)S(1)} collective-permute-done((bf16[16,640]{1,0:T(8,128)(2,1)S(1)}, bf16[16,640]{1,0:T(8,128)(2,1)S(1)}, u32[]{:S(2)}, u32[]{:S(2)}) %collective-permute-start.3) | collective-permute-done | bytes 20512 | tf_op jit(solution)/shard_map/ppermute | solution.py:22
  87.8 0.7 merge.1
  88.5 0.0 collective-permute-done.4.from_near
  88.5 0.0 collective-permute-done.5.from_far
  88.5 16.0 %all-to-all-start.2 = ((bf16[6,16,640]{2,1,0:T(8,128)(2,1)}), bf16[6,16,640]{2,1,0:T(8,128)(2,1)S(1)}, u32[]{:S(2)}, u32[]{:S(2)}) async-start(bf16[6,16,640]{2,1,0:T(8,128)(2,1)} %merge.1), calls=%async_computation.2 | async-start | bytes 245760 | tf_op jit(solution)/shard_map/all_to_all | solution.py:369
  104.5 0.0 copy-done.5
  104.5 0.4 own_part.1.part_own
  104.9 1.6 %final.1 = bf16[512,512]{1,0:T(8,128)(2,1)} custom-call(f32[512,512]{1,0:T(8,128)S(1)} %own_part.1.part_own, bf16[512,512]{1,0:T(8,128)(2,1)S(1)} %collective-permute-done.4.from_near, bf16[512,512]{1,0:T(8,128)(2,1)S(1)} %collective-permute-done.5.from_far, f32[512,1]{1,0:T(8,128)S(1)} %copy.14.root, bf16[512,512]{1,0:T(8,128)(2,1)S(1)} %copy-done), custom_call_target="tpu_custom_call" | custom-call | flops 100000000 | bytes 1000000 | tf_op jit(solution)/shard_map/final/pallas_call | solution.py:322
  106.6 6.1 %all-to-all-done.2.refs_0_ = bf16[6,16,640]{2,1,0:T(8,128)(2,1)S(1)} async-done(((bf16[6,16,640]{2,1,0:T(8,128)(2,1)}), bf16[6,16,640]{2,1,0:T(8,128)(2,1)S(1)}, u32[]{:S(2)}, u32[]{:S(2)}) %all-to-all-start.2) | async-done | bytes 122912 | tf_op jit(solution)/shard_map/all_to_all | solution.py:369
  112.7 0.6 last_sum.1
  (3 shorter events, 0.1 us)
Async XLA Ops:
  0.6 24.6 %copy-start.9 = (s32[512]{0:T(512)S(1)}, s32[512]{0:T(512)}, u32[]{:S(2)}) copy-start(s32[512]{0:T(512)} %param.12) | copy-start | bytes 6148
  0.6 25.4 %copy-start.10 = (s32[4,6]{1,0:T(4,128)S(1)}, s32[4,6]{1,0:T(4,128)}, u32[]{:S(2)}) copy-start(s32[4,6]{1,0:T(4,128)} %param.10) | copy-start | bytes 292
  2.6 32.7 %collective-permute-start.1 = (bf16[512,512]{1,0:T(8,128)(2,1)S(1)}, bf16[512,512]{1,0:T(8,128)(2,1)S(1)}, u32[]{:S(2)}, u32[]{:S(2)}) collective-permute-start(bf16[512,512]{1,0:T(8,128)(2,1)S(1)} %multiply_convert_fusion.own), channel_id=1, source_target_pairs={{0,767},{1,2},{2,1},{3,4},{4,3},{5,6},{6,5},{7,8},{8,7},{9,10},{10... | collective-permute-start | bytes 1572872 | tf_op jit(solution)/shard_map/ppermute | solution.py:22
  6.9 29.0 %collective-permute-start = (bf16[512,512]{1,0:T(8,128)(2,1)S(1)}, bf16[512,512]{1,0:T(8,128)(2,1)S(1)}, u32[]{:S(2)}, u32[]{:S(2)}) collective-permute-start(bf16[512,512]{1,0:T(8,128)(2,1)S(1)} %multiply_convert_fusion.own), channel_id=1, source_target_pairs={{0,1},{1,0},{2,3},{3,2},{4,5},{5,4},{6,7},{7,6},{8,9},{9,8},{10,11... | collective-permute-start | bytes 1572872 | tf_op jit(solution)/shard_map/ppermute | solution.py:22
  26.1 1.0 copy-start.6
  27.0 0.9 copy-start.7
  28.0 8.7 %copy-start = (bf16[512,512]{1,0:T(8,128)(2,1)S(1)}, bf16[512,512]{1,0:T(8,128)(2,1)}, u32[]{:S(2)}) copy-start(bf16[512,512]{1,0:T(8,128)(2,1)} %weight.3) | copy-start | bytes 1572868
  28.0 8.7 %copy-start.1 = (bf16[512,512]{1,0:T(8,128)(2,1)S(1)}, bf16[512,512]{1,0:T(8,128)(2,1)}, u32[]{:S(2)}) copy-start(bf16[512,512]{1,0:T(8,128)(2,1)} %grad.1) | copy-start | bytes 1572868
  28.0 8.7 %copy-start.8 = (f32[512]{0:T(512)S(1)}, f32[512]{0:T(512)}, u32[]{:S(2)}) copy-start(f32[512]{0:T(512)} %param.9) | copy-start | bytes 6148
  34.5 0.8 copy-start.4
  35.9 0.8 copy-start.2
  36.7 1.0 copy-start.3
  41.2 3.5 %collective-permute-start.2 = (bf16[256,640]{1,0:T(8,128)(2,1)S(1)}, bf16[256,640]{1,0:T(8,128)(2,1)S(1)}, u32[]{:S(2)}, u32[]{:S(2)}) collective-permute-start(bf16[256,640]{1,0:T(8,128)(2,1)S(1)} %get-tuple-element.27), channel_id=1, source_target_pairs={{0,24},{24,0},{1,25},{25,1},{2,26},{26,2},{3,27},{27,3},{4,28},{28... | collective-permute-start | bytes 983048 | tf_op jit(solution)/shard_map/ppermute | solution.py:22
  45.5 20.7 %all-to-all-start = ((bf16[8,32,640]{2,1,0:T(8,128)(2,1)}), bf16[8,32,640]{2,1,0:T(8,128)(2,1)S(1)}, u32[]{:S(2)}, u32[]{:S(2)}) async-start(bf16[8,32,640]{2,1,0:T(8,128)(2,1)} %bitcast.5), calls=%async_computation | async-start | bytes 655360 | tf_op jit(solution)/shard_map/all_to_all | solution.py:361
  52.6 51.9 %copy-start.5 = (bf16[512,512]{1,0:T(8,128)(2,1)S(1)}, bf16[512,512]{1,0:T(8,128)(2,1)}, u32[]{:S(2)}) copy-start(bf16[512,512]{1,0:T(8,128)(2,1)} %copy-done.4) | copy-start | bytes 1572868
  54.3 34.2 %collective-permute-start.4 = (bf16[512,512]{1,0:T(8,128)(2,1)}, bf16[512,512]{1,0:T(8,128)(2,1)S(1)}, u32[]{:S(2)}, u32[]{:S(2)}) collective-permute-start(bf16[512,512]{1,0:T(8,128)(2,1)} %get-tuple-element.33), channel_id=1, source_target_pairs={{0,1},{1,0},{2,3},{3,2},{4,5},{5,4},{6,7},{7,6},{8,9},{9,8},{10,11... | collective-permute-start | bytes 1572872 | tf_op jit(solution)/shard_map/ppermute | solution.py:22
  58.7 29.9 %collective-permute-start.5 = (bf16[512,512]{1,0:T(8,128)(2,1)}, bf16[512,512]{1,0:T(8,128)(2,1)S(1)}, u32[]{:S(2)}, u32[]{:S(2)}) collective-permute-start(bf16[512,512]{1,0:T(8,128)(2,1)} %get-tuple-element.34), channel_id=1, source_target_pairs={{0,767},{1,2},{2,1},{3,4},{4,3},{5,6},{6,5},{7,8},{8,7},{9,10},{10... | collective-permute-start | bytes 1572872 | tf_op jit(solution)/shard_map/ppermute | solution.py:22
  78.5 9.3 %collective-permute-start.3 = (bf16[16,640]{1,0:T(8,128)(2,1)S(1)}, bf16[16,640]{1,0:T(8,128)(2,1)S(1)}, u32[]{:S(2)}, u32[]{:S(2)}) collective-permute-start(bf16[16,640]{1,0:T(8,128)(2,1)S(1)} %get-tuple-element.31), channel_id=1, source_target_pairs={{0,53},{1,52},{2,51},{3,50},{4,49},{5,48},{48,5},{49,4},{50,3},{51... | collective-permute-start | bytes 61448 | tf_op jit(solution)/shard_map/ppermute | solution.py:22
  88.5 24.2 %all-to-all-start.2 = ((bf16[6,16,640]{2,1,0:T(8,128)(2,1)}), bf16[6,16,640]{2,1,0:T(8,128)(2,1)S(1)}, u32[]{:S(2)}, u32[]{:S(2)}) async-start(bf16[6,16,640]{2,1,0:T(8,128)(2,1)} %merge.1), calls=%async_computation.2 | async-start | bytes 245760 | tf_op jit(solution)/shard_map/all_to_all | solution.py:369

commit v6 on v4

--- a/solution.py
+++ b/solution.py
@@ -336,7 +336,6 @@
     from_near = permute(part_near, NODE, near_partner)
     ny, nx, nzl = (lax.axis_size(n) for n in ("y", "x", "zl"))
     chip = (wkeep.astype(f32) + got.astype(f32)).astype(bf16)
-    part_far, chip = lax.optimization_barrier((part_far, chip))
     from_far = permute(part_far, NODE, far_partner)
     blocks = lax.all_to_all(chip.reshape(ny, -1, width + 128), "y", 0, 0)
     own_t, from_near = lax.optimization_barrier((own_t, from_near))

time: 107 us -> 110 us (1.028)
  waiting for transfers between devices: 21.5 us -> 28.2 us
  blocking collectives: 13.6 us -> 8.51 us
  starting transfers between devices: 49.1 us -> 50.8 us
    all_to_all x1, waiting for transfers between devices: 2.69 us -> 9.93 us  [local(): blocks = lax.all_to_all(chip.reshape(ny, -1, width + 128), 'y', 0, 0)]
    all_to_all x1, blocking collectives: 13.6 us -> 8.51 us  [local(): blocks = lax.all_to_all(spread(blocks, 1, nx), 'x', 0, 0)]
    ppermute x6, starting transfers between devices: 35.8 us -> 39.2 us  [permute(): lax.ppermute(array, axes, [(i, route(i) % peers) for i in range(peers)])]
    all_to_all x1, starting transfers between devices: 5.75 us -> 3.89 us  [local(): blocks = lax.all_to_all(blocks, 'zl', 0, 0)]
  transfers between devices with their start and end apart: 8 -> 8, of which waited for: 5 -> 5; matrix products, arithmetic and copies ran while one was open for 2% -> 2% of each run, Pallas kernels for 11% -> 10%
where the time goes in v6:
time: 110 us
  starting transfers between devices  50.8 us (46%)
  waiting for transfers between devices  28.2 us (26%)
  Pallas kernels  16.3 us (15%)
  blocking collectives  8.51 us (8%)
  other arithmetic  2.79 us (3%)
  local copies, waits for them, and re-layouts  2.09 us (2%)
    ppermute x6, starting transfers between devices, permute(): lax.ppermute(array, axes, [(i, route(i) % peers) for i in range(peers)])  39.2 us
    ppermute x6, waiting for transfers between devices, permute(): lax.ppermute(array, axes, [(i, route(i) % peers) for i in range(peers)])  11.9 us
    all_to_all x1, waiting for transfers between devices, local(): blocks = lax.all_to_all(chip.reshape(ny, -1, width + 128), 'y', 0, 0)  9.93 us
    all_to_all x1, blocking collectives, local(): blocks = lax.all_to_all(spread(blocks, 1, nx), 'x', 0, 0)  8.51 us
    all_to_all x1, starting transfers between devices, local(): blocks = lax.all_to_all(chip.reshape(ny, -1, width + 128), 'y', 0, 0)  7.66 us
    pallas_call x1, Pallas kernels, build_adjacency(): pl.pallas_call(adjacency_kernel, grid=(tiles,), in_specs=[pl.BlockSpec(me...  6.49 us
    all_to_all x1, waiting for transfers between devices, local(): blocks = lax.all_to_all(blocks, 'zl', 0, 0)  6.34 us
    pallas_call x1, Pallas kernels, forward(): pl.pallas_call(forward_kernel, in_specs=[pl.BlockSpec(memory_space=pltpu....  4.33 us
  transfers between devices with their start and end apart: 8, of which 5 were waited for; matrix products, arithmetic and copies ran while one was open for 2% of the time, Pallas kernels for 10%

profile of v6, /device:TPU:8, one launch (start us, length us, event | category | flops | bytes accessed | tf_op | source)
XLA Modules:
  0.0 109.5 jit_solution(17078710652083523091)
XLA Ops:
  0.6 0.0 copy-start.6
  0.6 0.0 copy-start.7
  0.7 0.7 add_rsqrt_fusion
  1.4 1.2 %multiply_convert_fusion.own = bf16[512,512]{1,0:T(8,128)(2,1)S(1)} fusion(bf16[512,512]{1,0:T(8,128)(2,1)} %param.7, f32[512]{0:T(512)S(1)} %add_rsqrt_fusion), kind=kLoop, calls=%fused_computation | loop fusion | flops 786432 | bytes 1050624 | tf_op jit(solution)/shard_map/convert_element_type | solution.py:327
  2.6 16.1 %collective-permute-start.1 = (bf16[512,512]{1,0:T(8,128)(2,1)S(1)}, bf16[512,512]{1,0:T(8,128)(2,1)S(1)}, u32[]{:S(2)}, u32[]{:S(2)}) collective-permute-start(bf16[512,512]{1,0:T(8,128)(2,1)S(1)} %multiply_convert_fusion.own), channel_id=1, source_target_pairs={{0,767},{1,2},{2,1},{3,4},{4,3},{5,6},{6,5},{7,8},{8,7},{9,10},{10... | collective-permute-start | bytes 1572872 | tf_op jit(solution)/shard_map/ppermute | solution.py:22
  18.7 1.9 %collective-permute-start = (bf16[512,512]{1,0:T(8,128)(2,1)S(1)}, bf16[512,512]{1,0:T(8,128)(2,1)S(1)}, u32[]{:S(2)}, u32[]{:S(2)}) collective-permute-start(bf16[512,512]{1,0:T(8,128)(2,1)S(1)} %multiply_convert_fusion.own), channel_id=1, source_target_pairs={{0,1},{1,0},{2,3},{3,2},{4,5},{5,4},{6,7},{7,6},{8,9},{9,8},{10,11... | collective-permute-start | bytes 1572872 | tf_op jit(solution)/shard_map/ppermute | solution.py:22
  20.7 0.1 copy.14.root
  20.8 1.0 copy.12.nbr_ref
  21.8 0.0 copy-done.6
  21.8 0.1 copy.13.cnt_ref
  22.0 0.0 copy-done.7
  22.0 0.0 copy-start
  22.0 0.0 copy-start.4
  22.1 0.0 copy-start.5
  22.1 6.5 %adjacency.1 = (bf16[512,1536]{1,0:T(8,128)(2,1)S(1)}, bf16[1024,512]{1,0:T(8,128)(2,1)S(1)}, bf16[512,512]{1,0:T(8,128)(2,1)S(1)}) custom-call(s32[4,6]{1,0:T(4,128)S(1)} %add_select_fusion.slot_ref, s32[512,30]{1,0:T(8,128)S(1)} %copy.12.nbr_ref, s32[512,1]{1,0:T(8,128)S(1)} %copy.13.cnt_ref), custom_call_target="tpu_custom_call" | custom-call | flops 1000000000 | bytes 8000000 | tf_op jit(solution)/shard_map/adjacency/pallas_call | solution.py:75
  28.6 1.9 %collective-permute-done.1.far = bf16[512,512]{1,0:T(8,128)(2,1)S(1)} collective-permute-done((bf16[512,512]{1,0:T(8,128)(2,1)S(1)}, bf16[512,512]{1,0:T(8,128)(2,1)S(1)}, u32[]{:S(2)}, u32[]{:S(2)}) %collective-permute-start.1) | collective-permute-done | bytes 524320 | tf_op jit(solution)/shard_map/ppermute | solution.py:22
  30.5 8.3 %collective-permute-done.near = bf16[512,512]{1,0:T(8,128)(2,1)S(1)} collective-permute-done((bf16[512,512]{1,0:T(8,128)(2,1)S(1)}, bf16[512,512]{1,0:T(8,128)(2,1)S(1)}, u32[]{:S(2)}, u32[]{:S(2)}) %collective-permute-start) | collective-permute-done | bytes 524320 | tf_op jit(solution)/shard_map/ppermute | solution.py:22
  38.7 0.0 copy-done
  38.7 0.0 copy-done.4
  38.7 0.0 copy-done.5
  38.7 4.3 %forward.1 = (bf16[512,512]{1,0:T(8,128)(2,1)}, bf16[256,640]{1,0:T(8,128)(2,1)S(1)}, bf16[256,640]{1,0:T(8,128)(2,1)S(1)}, bf16[512,512]{1,0:T(8,128)(2,1)S(1)}...) custom-call(s32[1]{0:T(128)} %bitcast.core_ref, bf16[512,1536]{1,0:T(8,128)(2,1)S(1)} %get-tuple-element.23.adj, ...), custom_call_target="tpu_custom_call" | custom-call | flops 1000000000 | bytes 10000000 | tf_op jit(solution)/shard_map/forward/pallas_call | solution.py:149
  43.1 1.9 %collective-permute-start.2 = (bf16[256,640]{1,0:T(8,128)(2,1)S(1)}, bf16[256,640]{1,0:T(8,128)(2,1)S(1)}, u32[]{:S(2)}, u32[]{:S(2)}) collective-permute-start(bf16[256,640]{1,0:T(8,128)(2,1)S(1)} %get-tuple-element.27), channel_id=1, source_target_pairs={{0,24},{24,0},{1,25},{25,1},{2,26},{26,2},{3,27},{27,3},{4,28},{28... | collective-permute-start | bytes 983048 | tf_op jit(solution)/shard_map/ppermute | solution.py:22
  45.0 1.9 %collective-permute-start.3 = (bf16[512,512]{1,0:T(8,128)(2,1)S(1)}, bf16[512,512]{1,0:T(8,128)(2,1)S(1)}, u32[]{:S(2)}, u32[]{:S(2)}) collective-permute-start(bf16[512,512]{1,0:T(8,128)(2,1)S(1)} %get-tuple-element.29), channel_id=1, source_target_pairs={{0,1},{1,0},{2,3},{3,2},{4,5},{5,4},{6,7},{7,6},{8,9},{9,8},{10,11... | collective-permute-start | bytes 1572872 | tf_op jit(solution)/shard_map/ppermute | solution.py:22
  46.9 9.4 %collective-permute-start.5 = (bf16[512,512]{1,0:T(8,128)(2,1)}, bf16[512,512]{1,0:T(8,128)(2,1)}, u32[]{:S(2)}, u32[]{:S(2)}) collective-permute-start(bf16[512,512]{1,0:T(8,128)(2,1)} %get-tuple-element.37), channel_id=1, source_target_pairs={{0,767},{1,2},{2,1},{3,4},{4,3},{5,6},{6,5},{7,8},{8,7},{9,10},{10... | collective-permute-start | bytes 1572872 | tf_op jit(solution)/shard_map/ppermute | solution.py:22
  56.3 0.0 collective-permute-done.2
  56.3 0.8 add_convert_fusion
  57.1 7.7 %all-to-all-start = ((bf16[8,32,640]{2,1,0:T(8,128)(2,1)}), bf16[8,32,640]{2,1,0:T(8,128)(2,1)}, u32[]{:S(2)}, u32[]{:S(2)}) async-start(bf16[8,32,640]{2,1,0:T(8,128)(2,1)} %bitcast.4), calls=%async_computation | async-start | bytes 655360 | tf_op jit(solution)/shard_map/all_to_all | solution.py:340
  64.8 0.0 collective-permute-done.3.from_near
  64.8 0.0 copy-start.2
  64.8 0.8 copy-done.2
  65.6 0.4 own_part.1.part_own
  66.0 0.0 copy-start.1
  66.0 0.0 copy-start.3
  66.0 9.9 %all-to-all-done.blocks = bf16[8,32,640]{2,1,0:T(8,128)(2,1)} async-done(((bf16[8,32,640]{2,1,0:T(8,128)(2,1)}), bf16[8,32,640]{2,1,0:T(8,128)(2,1)}, u32[]{:S(2)}, u32[]{:S(2)}) %all-to-all-start) | async-done | bytes 327712 | tf_op jit(solution)/shard_map/all_to_all | solution.py:340
  76.0 1.0 spread.1
  77.0 8.5 %all_to_all.15.blocks = bf16[4,32,640]{2,1,0:T(8,128)(2,1)S(1)} all-to-all(bf16[4,32,640]{2,1,0:T(8,128)(2,1)S(1)} %spread.1), channel_id=1, replica_groups=mesh['y'=8,'zh'=2,'core'=2,'x'=4,'zl'=6] {'x'}, dimensions={0} | all-to-all | bytes 327680 | tf_op jit(solution)/shard_map/all_to_all | solution.py:344
  85.5 8.0 %collective-permute-start.4 = (bf16[16,640]{1,0:T(8,128)(2,1)S(1)}, bf16[16,640]{1,0:T(8,128)(2,1)S(1)}, u32[]{:S(2)}, u32[]{:S(2)}) collective-permute-start(bf16[16,640]{1,0:T(8,128)(2,1)S(1)} %get-tuple-element.36), channel_id=1, source_target_pairs={{0,53},{1,52},{2,51},{3,50},{4,49},{5,48},{48,5},{49,4},{50,3},{51... | collective-permute-start | bytes 61448 | tf_op jit(solution)/shard_map/ppermute | solution.py:22
  93.6 1.7 %collective-permute-done.4.pair = bf16[16,640]{1,0:T(8,128)(2,1)S(1)} collective-permute-done((bf16[16,640]{1,0:T(8,128)(2,1)S(1)}, bf16[16,640]{1,0:T(8,128)(2,1)S(1)}, u32[]{:S(2)}, u32[]{:S(2)}) %collective-permute-start.4) | collective-permute-done | bytes 20512 | tf_op jit(solution)/shard_map/ppermute | solution.py:22
  95.3 0.7 merge.1
  96.0 0.0 collective-permute-done.5.from_far
  96.0 3.9 %all-to-all-start.2 = ((bf16[6,16,640]{2,1,0:T(8,128)(2,1)}), bf16[6,16,640]{2,1,0:T(8,128)(2,1)S(1)}, u32[]{:S(2)}, u32[]{:S(2)}) async-start(bf16[6,16,640]{2,1,0:T(8,128)(2,1)} %merge.1), calls=%async_computation.2 | async-start | bytes 245760 | tf_op jit(solution)/shard_map/all_to_all | solution.py:350
  99.9 0.0 copy-done.1
  99.9 0.0 copy-done.3
  99.9 2.7 %final.1 = bf16[512,512]{1,0:T(8,128)(2,1)} custom-call(f32[512,512]{1,0:T(8,128)S(1)} %own_part.1.part_own, bf16[512,512]{1,0:T(8,128)(2,1)S(1)} %copy-done.3, bf16[512,512]{1,0:T(8,128)(2,1)} %collective-permute-done.5.from_far, f32[512,1]{1,0:T(8,128)S(1)} %copy.14.root, bf16[512,512]{1,0:T(8,128)(2,1)S(1)} %copy-done.1), custom_call_target="tpu_custom_call" | custom-call | flops 100000000 | bytes 1000000 | tf_op jit(solution)/shard_map/final/pallas_call | solution.py:303
  102.5 6.3 %all-to-all-done.2.refs_0_ = bf16[6,16,640]{2,1,0:T(8,128)(2,1)S(1)} async-done(((bf16[6,16,640]{2,1,0:T(8,128)(2,1)}), bf16[6,16,640]{2,1,0:T(8,128)(2,1)S(1)}, u32[]{:S(2)}, u32[]{:S(2)}) %all-to-all-start.2) | async-done | bytes 122912 | tf_op jit(solution)/shard_map/all_to_all | solution.py:350
  108.9 0.6 last_sum.1
  (2 shorter events, 0.0 us)
Async XLA Ops:
  0.6 21.2 %copy-start.6 = (s32[512]{0:T(512)S(1)}, s32[512]{0:T(512)}, u32[]{:S(2)}) copy-start(s32[512]{0:T(512)} %param.12) | copy-start | bytes 6148
  0.6 21.4 %copy-start.7 = (s32[4,6]{1,0:T(4,128)S(1)}, s32[4,6]{1,0:T(4,128)}, u32[]{:S(2)}) copy-start(s32[4,6]{1,0:T(4,128)} %param.10) | copy-start | bytes 292
  2.6 27.9 %collective-permute-start.1 = (bf16[512,512]{1,0:T(8,128)(2,1)S(1)}, bf16[512,512]{1,0:T(8,128)(2,1)S(1)}, u32[]{:S(2)}, u32[]{:S(2)}) collective-permute-start(bf16[512,512]{1,0:T(8,128)(2,1)S(1)} %multiply_convert_fusion.own), channel_id=1, source_target_pairs={{0,767},{1,2},{2,1},{3,4},{4,3},{5,6},{6,5},{7,8},{8,7},{9,10},{10... | collective-permute-start | bytes 1572872 | tf_op jit(solution)/shard_map/ppermute | solution.py:22
  18.7 20.0 %collective-permute-start = (bf16[512,512]{1,0:T(8,128)(2,1)S(1)}, bf16[512,512]{1,0:T(8,128)(2,1)S(1)}, u32[]{:S(2)}, u32[]{:S(2)}) collective-permute-start(bf16[512,512]{1,0:T(8,128)(2,1)S(1)} %multiply_convert_fusion.own), channel_id=1, source_target_pairs={{0,1},{1,0},{2,3},{3,2},{4,5},{5,4},{6,7},{7,6},{8,9},{9,8},{10,11... | collective-permute-start | bytes 1572872 | tf_op jit(solution)/shard_map/ppermute | solution.py:22
  22.0 16.7 %copy-start = (bf16[512,512]{1,0:T(8,128)(2,1)S(1)}, bf16[512,512]{1,0:T(8,128)(2,1)}, u32[]{:S(2)}) copy-start(bf16[512,512]{1,0:T(8,128)(2,1)} %weight.3) | copy-start | bytes 1572868
  22.0 16.7 %copy-start.4 = (bf16[512,512]{1,0:T(8,128)(2,1)S(1)}, bf16[512,512]{1,0:T(8,128)(2,1)}, u32[]{:S(2)}) copy-start(bf16[512,512]{1,0:T(8,128)(2,1)} %grad.1) | copy-start | bytes 1572868
  22.1 16.7 %copy-start.5 = (f32[512]{0:T(512)S(1)}, f32[512]{0:T(512)}, u32[]{:S(2)}) copy-start(f32[512]{0:T(512)} %param.9) | copy-start | bytes 6148
  43.1 13.2 %collective-permute-start.2 = (bf16[256,640]{1,0:T(8,128)(2,1)S(1)}, bf16[256,640]{1,0:T(8,128)(2,1)S(1)}, u32[]{:S(2)}, u32[]{:S(2)}) collective-permute-start(bf16[256,640]{1,0:T(8,128)(2,1)S(1)} %get-tuple-element.27), channel_id=1, source_target_pairs={{0,24},{24,0},{1,25},{25,1},{2,26},{26,2},{3,27},{27,3},{4,28},{28... | collective-permute-start | bytes 983048 | tf_op jit(solution)/shard_map/ppermute | solution.py:22
  45.0 19.8 %collective-permute-start.3 = (bf16[512,512]{1,0:T(8,128)(2,1)S(1)}, bf16[512,512]{1,0:T(8,128)(2,1)S(1)}, u32[]{:S(2)}, u32[]{:S(2)}) collective-permute-start(bf16[512,512]{1,0:T(8,128)(2,1)S(1)} %get-tuple-element.29), channel_id=1, source_target_pairs={{0,1},{1,0},{2,3},{3,2},{4,5},{5,4},{6,7},{7,6},{8,9},{9,8},{10,11... | collective-permute-start | bytes 1572872 | tf_op jit(solution)/shard_map/ppermute | solution.py:22
  46.9 49.0 %collective-permute-start.5 = (bf16[512,512]{1,0:T(8,128)(2,1)}, bf16[512,512]{1,0:T(8,128)(2,1)}, u32[]{:S(2)}, u32[]{:S(2)}) collective-permute-start(bf16[512,512]{1,0:T(8,128)(2,1)} %get-tuple-element.37), channel_id=1, source_target_pairs={{0,767},{1,2},{2,1},{3,4},{4,3},{5,6},{6,5},{7,8},{8,7},{9,10},{10... | collective-permute-start | bytes 1572872 | tf_op jit(solution)/shard_map/ppermute | solution.py:22
  57.1 18.9 %all-to-all-start = ((bf16[8,32,640]{2,1,0:T(8,128)(2,1)}), bf16[8,32,640]{2,1,0:T(8,128)(2,1)}, u32[]{:S(2)}, u32[]{:S(2)}) async-start(bf16[8,32,640]{2,1,0:T(8,128)(2,1)} %bitcast.4), calls=%async_computation | async-start | bytes 655360 | tf_op jit(solution)/shard_map/all_to_all | solution.py:340
  64.8 0.8 copy-start.2
  66.0 33.9 %copy-start.1 = (bf16[512,512]{1,0:T(8,128)(2,1)S(1)}, bf16[512,512]{1,0:T(8,128)(2,1)}, u32[]{:S(2)}) copy-start(bf16[512,512]{1,0:T(8,128)(2,1)} %weight.3) | copy-start | bytes 1572868
  66.0 33.8 %copy-start.3 = (bf16[512,512]{1,0:T(8,128)(2,1)S(1)}, bf16[512,512]{1,0:T(8,128)(2,1)}, u32[]{:S(2)}) copy-start(bf16[512,512]{1,0:T(8,128)(2,1)} %copy-done.2) | copy-start | bytes 1572868
  85.5 9.8 %collective-permute-start.4 = (bf16[16,640]{1,0:T(8,128)(2,1)S(1)}, bf16[16,640]{1,0:T(8,128)(2,1)S(1)}, u32[]{:S(2)}, u32[]{:S(2)}) collective-permute-start(bf16[16,640]{1,0:T(8,128)(2,1)S(1)} %get-tuple-element.36), channel_id=1, source_target_pairs={{0,53},{1,52},{2,51},{3,50},{4,49},{5,48},{48,5},{49,4},{50,3},{51... | collective-permute-start | bytes 61448 | tf_op jit(solution)/shard_map/ppermute | solution.py:22
  96.0 12.9 %all-to-all-start.2 = ((bf16[6,16,640]{2,1,0:T(8,128)(2,1)}), bf16[6,16,640]{2,1,0:T(8,128)(2,1)S(1)}, u32[]{:S(2)}, u32[]{:S(2)}) async-start(bf16[6,16,640]{2,1,0:T(8,128)(2,1)} %merge.1), calls=%async_computation.2 | async-start | bytes 245760 | tf_op jit(solution)/shard_map/all_to_all | solution.py:350
